TPU v7x, 32 devices: a whole 2x2x4 slice. The times are simulated.
32 devices in a mesh: tm: 8 (over z, y), pair: 4 (over x, core).
Axes of the slice: x: 2, y: 2, z: 4, core: 2. Of those that a mesh axis runs over, the one named last changes fastest.
Arguments:
- x_path: bfloat16 [8, 4096, 512], P('pair', 'tm'), parts along dimension 0, may hold values from -0.19921875 to 0.19921875
- x_anchor: bfloat16 [8, 512], P('pair'), parts along dimension 0, may hold values from -0.19921875 to 0.19921875
- y_steps: bfloat16 [8, 1024, 512], P('pair', 'tm'), parts along dimension 0, may hold values from -0.14941406 to 0.14941406
- left_in: float32 [16, 4096], P('pair', 'tm'), parts along dimension 0, may hold values from 0.5 to 1.5
- bottom_in: float32 [16, 1024], P('pair', 'tm'), parts along dimension 0, may hold values from 0.5 to 1.5
- corner_in: float32 [16, 8], P('pair', 'tm'), parts along dimension 0, may hold values from 0.5 to 1.5
Outputs:
- right_out: float32 [16, 4096], P('pair', 'tm'), parts along dimension 0
- top_out: float32 [16, 6144], P('pair', 'tm'), parts along dimension 0
There are 4 independent parts, one for each index of `pair`. A program takes and returns all parts, laid end to end along the dimension named above; each array names one. Nothing has to cross between parts.
All inputs are finite; a program needn't handle non-finite values.
Results may differ from a plain program's by a relative error of at most 0.00094.
Values may be sent and summed in bfloat16 or wider, within the bound.
No kernel may reach another device: no remote copies, remote signals or barrier semaphores. Data moves between devices by JAX's collectives and lax.ppermute only.
A program may use at most 64 MiB of HBM per device.

v0:
```python
import functools

import jax
import jax.numpy as jnp
from jax import lax
from jax.experimental import pallas as pl
from jax.experimental.pallas import tpu as pltpu
from jax.sharding import PartitionSpec as P

TICKS = 6
PASSES = 4
SUB = 8


def shifted(x, axis, by):
    count = lax.axis_size(axis)
    pairs = [(i, i + by) for i in range(count) if 0 <= i + by < count]
    return lax.ppermute(x, axis, pairs)


def passed_along(x, axis, by):
    count = lax.axis_size(axis)
    return lax.ppermute(x, axis, [(i, (i + by) % count) for i in range(count)])


def two_halves(x):
    high = x.astype(jnp.bfloat16)
    low = (x - high.astype(jnp.float32)).astype(jnp.bfloat16)
    return jnp.concatenate([high, low], axis=1)


def tick_kernel(
    last, start_ref, dx_ref, y_ref, bottom_ref, before_ref, left_ref, out_ref, top_ref, products_ref
):
    series_x, block_len, channels = dx_ref.shape
    series_y, tile, _ = y_ref.shape
    pairs = series_x * series_y
    levels = block_len // tile
    groups = tile // SUB

    y_all = y_ref[...].reshape(series_y * tile, channels)
    for m in range(series_x):
        both = lax.dot_general(
            dx_ref[m], y_all, (((1,), (1,)), ((), ())), preferred_element_type=jnp.float32
        )
        for n in range(series_y):
            products_ref[m * series_y + n] = both[:, n * tile : (n + 1) * tile]

    row = lax.broadcasted_iota(jnp.int32, (2 * tile, tile), 0) % tile
    col = lax.broadcasted_iota(jnp.int32, (2 * tile, tile), 1)
    strict = (row < col).astype(jnp.float32).astype(jnp.bfloat16)
    inclusive = (row <= col).astype(jnp.float32).astype(jnp.bfloat16)
    ones = jnp.ones((2 * tile, tile), jnp.bfloat16)
    edge_sums = jnp.concatenate([strict, inclusive], axis=1)
    sub = lax.broadcasted_iota(jnp.int32, (SUB, tile), 0)
    lane = lax.broadcasted_iota(jnp.int32, (SUB, tile), 1)
    at_start = start_ref[0] == 1

    def sum_before(total):
        out = jnp.where(sub >= 1, pltpu.roll(total, 1, 0), 0.0)
        step = 1
        while step < SUB - 1:
            out = out + jnp.where(sub >= step, pltpu.roll(out, step, 0), 0.0)
            step *= 2
        return out

    def over_sublanes(x):
        step = SUB // 2
        while step:
            x = x + pltpu.roll(x, step, 0)
            step //= 2
        return x

    def dot(a, b):
        return jnp.dot(a, b, preferred_element_type=jnp.float32)

    bottom, bottom_shift, corner = [], [], []
    for p in range(pairs):
        b = jnp.broadcast_to(bottom_ref[p : p + 1, :], (SUB, tile))
        b = jnp.where(at_start, 1.0, b)
        c = jnp.broadcast_to(before_ref[p : p + 1, tile - 1 : tile], (SUB, tile))
        c = jnp.where(at_start, 1.0, c)
        bottom.append(b)
        corner.append(c)
        bottom_shift.append(jnp.where(lane == 0, c, pltpu.roll(b, 1, 1)))

    for r in range(levels):
        edge, end = [], []
        for p in range(pairs):
            left = [left_ref[p, r, j] for j in range(groups)]
            first = jnp.where(sub == 0, corner[p], pltpu.roll(left[-1], 1, 0))
            edge.append([x - corner[p] for x in [first] + left[:-1]])
            end.append(jnp.broadcast_to(left[-1][SUB - 1 : SUB, :], (SUB, tile)))
        node = [[e + bottom_shift[p] for e in edge[p]] for p in range(pairs)]
        for sweep in range(PASSES):
            weighted = [
                [
                    node[p][j] * products_ref[p, pl.ds(r * tile + j, SUB, stride=groups), :]
                    for j in range(groups)
                ]
                for p in range(pairs)
            ]
            if sweep == PASSES - 1:
                break
            for p in range(pairs):
                along = dot(two_halves(jnp.concatenate(weighted[p], axis=0)), strict)
                along = [along[j * SUB : (j + 1) * SUB] for j in range(groups)]
                running = [None, along[0]]
                for j in range(1, groups):
                    running.append(running[-1] + along[j])
                offset = sum_before(running[-1]) + bottom_shift[p]
                node[p] = [edge[p][0] + offset] + [
                    (running[j] + edge[p][j]) + offset for j in range(1, groups)
                ]
        for p in range(pairs):
            column = weighted[p]
            while len(column) > 1:
                column = [a + b for a, b in zip(column[::2], column[1::2])]
            column = over_sublanes(column[0])
            sums = dot(two_halves(column), edge_sums)
            lift = end[p] - corner[p]
            rows = dot(two_halves(jnp.concatenate(weighted[p], axis=0)), ones)
            rows = [rows[j * SUB : (j + 1) * SUB] for j in range(groups)]
            running = [rows[0]]
            for j in range(1, groups):
                running.append(running[-1] + rows[j])
            far = jnp.broadcast_to(bottom[p][:, tile - 1 : tile], (SUB, tile)) - corner[p]
            offset = sum_before(running[-1]) + far
            right = [left_ref[p, r, j] + (running[j] + offset) for j in range(groups)]
            if last:
                found = None
                for j in range(groups):
                    here = jnp.where(lane == sub * groups + j, right[j], 0.0)
                    found = here if found is None else found + here
                found = over_sublanes(found)
                out_ref[p : p + 1, r * tile : (r + 1) * tile] = found[0:1]
            else:
                for j in range(groups):
                    out_ref[p, r, j] = right[j]
            bottom[p] = bottom[p] + lift + sums[:, tile:]
            bottom_shift[p] = bottom_shift[p] + lift + sums[:, :tile]
            corner[p] = end[p]
    for p in range(pairs):
        top_ref[p : p + 1, :] = bottom[p][0:1]


def tick(start, dx, y, bottom, before, left, last):
    pairs, tile = bottom.shape
    block_len = dx.shape[1]
    vmem = pl.BlockSpec(memory_space=pltpu.VMEM)
    if last:
        left_out = jax.ShapeDtypeStruct((pairs, block_len), jnp.float32)
    else:
        left_out = jax.ShapeDtypeStruct(left.shape, jnp.float32)
    return pl.pallas_call(
        functools.partial(tick_kernel, last),
        out_shape=(left_out, jax.ShapeDtypeStruct((pairs, tile), jnp.float32)),
        in_specs=[pl.BlockSpec(memory_space=pltpu.SMEM)] + [vmem] * 5,
        out_specs=(vmem, vmem),
        scratch_shapes=[pltpu.VMEM((pairs, block_len, tile), jnp.float32)],
        name="tick_last" if last else "tick",
    )(start, dx, y, bottom, before, left)


def local(x_path, x_anchor, y_steps, left_in, bottom_in, corner_in):
    series_x, block_len, channels = x_path.shape
    series_y, tile, _ = y_steps.shape
    pairs = series_x * series_y
    levels = block_len // tile
    groups = tile // SUB
    at_start = lax.axis_index("tm") == 0
    start = at_start.astype(jnp.int32).reshape(1)
    received = shifted(x_path[:, -1:, :], "tm", 1)
    before = jnp.where(at_start, x_anchor[:, None, :], received)
    earlier = jnp.concatenate([before, x_path[:, :-1, :]], axis=1)
    dx = (x_path.astype(jnp.float32) - earlier.astype(jnp.float32)).astype(jnp.bfloat16)
    left = left_in.reshape(pairs, levels, SUB, groups).transpose(0, 1, 3, 2)
    left = jnp.broadcast_to(left[..., None], left.shape + (tile,))
    bottom = bottom_in
    previous = jnp.broadcast_to(corner_in, (pairs, tile))
    y_now = y_steps
    tops = []
    for t in range(TICKS):
        y_next = passed_along(y_now, "tm", 1) if t < TICKS - 1 else None
        left, top = tick(start, dx, y_now, bottom, previous, left, t == TICKS - 1)
        tops.append(top)
        if t < TICKS - 1:
            previous, bottom = bottom, shifted(top, "tm", 1)
            y_now = y_next
    return left, jnp.concatenate(tops, axis=1)


def solution(mesh):
    placed = (
        P("pair", "tm", None),
        P("pair", None),
        P("pair", "tm", None),
        P("pair", "tm"),
        P("pair", "tm"),
        P("pair", "tm"),
    )
    return jax.shard_map(
        local,
        mesh=mesh,
        in_specs=placed,
        out_specs=(P("pair", "tm"), P("pair", "tm")),
        check_vma=False,
    )
```

profile of v0, /device:TPU:24, one launch (start us, length us, event | category | flops | bytes accessed | tf_op | source)
XLA Modules:
  0.0 107.7 jit_solution(15448387641098407461)
XLA Ops:
  0.6 1.6 %collective-permute-start.1 = (bf16[2,128,512]{2,1,0:T(8,128)(2,1)}, bf16[2,128,512]{2,1,0:T(8,128)(2,1)S(1)}, u32[]{:S(2)}, u32[]{:S(2)}) collective-permute-start(bf16[2,128,512]{2,1,0:T(8,128)(2,1)} %y_ref.1), channel_id=1, source_target_pairs={{0,4},{4,8},{8,12},{12,16},{16,20},{20,24},{24,28},{28,0},{1,5},{5... | collective-permute-start | bytes 786440 | tf_op jit(solution)/shard_map/ppermute | solution.py:23
  2.2 7.6 %collective-permute-done.1.y_ref = bf16[2,128,512]{2,1,0:T(8,128)(2,1)S(1)} collective-permute-done((bf16[2,128,512]{2,1,0:T(8,128)(2,1)}, bf16[2,128,512]{2,1,0:T(8,128)(2,1)S(1)}, u32[]{:S(2)}, u32[]{:S(2)}) %collective-permute-start.1) | collective-permute-done | bytes 262176 | tf_op jit(solution)/shard_map/ppermute | solution.py:23
  10.5 7.5 %collective-permute-done.2.y_ref = bf16[2,128,512]{2,1,0:T(8,128)(2,1)S(1)} collective-permute-done((bf16[2,128,512]{2,1,0:T(8,128)(2,1)S(1)}, bf16[2,128,512]{2,1,0:T(8,128)(2,1)S(1)}, u32[]{:S(2)}, u32[]{:S(2)}) %collective-permute-start.2) | collective-permute-done | bytes 262176 | tf_op jit(solution)/shard_map/ppermute | solution.py:23
  19.2 7.1 %collective-permute-start = (bf16[2,1,512]{2,1,0:T(2,128)(2,1)S(1)}, bf16[2,1,512]{2,1,0:T(2,128)(2,1)S(1)}, u32[]{:S(2)}, u32[]{:S(2)}) collective-permute-start(bf16[2,1,512]{2,1,0:T(2,128)(2,1)S(1)} %slice.6), channel_id=1, source_target_pairs={{0,4},{4,8},{8,12},{12,16},{16,20},{20,24},{24,28},{1,5},{5,9},{9,... | collective-permute-start | bytes 6152 | tf_op jit(solution)/shard_map/ppermute | solution.py:18
  26.3 0.8 reshape.15
  28.3 2.3 %collective-permute-start.4 = (bf16[2,128,512]{2,1,0:T(8,128)(2,1)S(1)}, bf16[2,128,512]{2,1,0:T(8,128)(2,1)S(1)}, u32[]{:S(2)}, u32[]{:S(2)}) collective-permute-start(bf16[2,128,512]{2,1,0:T(8,128)(2,1)S(1)} %collective-permute-done.3.y_ref), channel_id=1, source_target_pairs={{0,4},{4,8},{8,12},{12,16},{16,20},{20,24},{24,28},{28,0},{1,5},{5... | collective-permute-start | bytes 786440 | tf_op jit(solution)/shard_map/ppermute | solution.py:23
  30.6 3.1 %subtract_convert_fusion.dx_ref = bf16[2,512,512]{2,1,0:T(8,128)(2,1)} fusion(bf16[2,512,512]{2,1,0:T(8,128)(2,1)} %param.6, bf16[2,511,512]{2,1,0:T(8,128)(2,1)} %bitcast.5, bf16[2,1,512]{2,1,0:T(2,128)(2,1)S(1)} %broadcast_select_fusion), kind=kLoop, calls=%fused_computation | loop fusion | flops 3670016 | bytes 3145728 | tf_op jit(solution)/shard_map/convert_element_type | solution.py:176
  33.7 1.3 %broadcast_in_dim.19.left_ref = f32[4,4,16,8,128]{4,3,2,1,0:T(8,128)} broadcast(f32[4,4,16,8]{3,2,1,0:T(8,128)S(1)} %bitcast.6), dimensions={0,1,2,3} | broadcast | bytes 1056768 | tf_op jit(solution)/shard_map/broadcast_in_dim | solution.py:178
  35.7 5.8 %tick.5 = (f32[4,4,16,8,128]{4,3,2,1,0:T(8,128)}, f32[4,128]{1,0:T(4,128)}) custom-call(s32[1]{0:T(128)} %bitcast.start_ref, bf16[2,512,512]{2,1,0:T(8,128)(2,1)} %subtract_convert_fusion.dx_ref, bf16[2,128,512]{2,1,0:T(8,128)(2,1)} %y_ref.1, f32[4,128]{1,0:T(4,128)} %before_ref.1, f32[4,128]{1,0:T(4,128)} %broadcast_in_dim.18.before_ref, ...), custom_call_target="tpu_custom_call" | custom-call | tf_op jit(solution)/shard_map/tick/pallas_call | solution.py:155
  41.5 4.2 %collective-permute-start.6 = (f32[4,128]{1,0:T(4,128)}, f32[4,128]{1,0:T(4,128)S(1)}, u32[]{:S(2)}, u32[]{:S(2)}) collective-permute-start(f32[4,128]{1,0:T(4,128)} %get-tuple-element.14), channel_id=1, source_target_pairs={{0,4},{4,8},{8,12},{12,16},{16,20},{20,24},{24,28},{1,5},{5,9},{9,... | collective-permute-start | bytes 6152 | tf_op jit(solution)/shard_map/ppermute | solution.py:18
  46.4 1.7 %collective-permute-done.6.bottom_ref.before_ref = f32[4,128]{1,0:T(4,128)S(1)} collective-permute-done((f32[4,128]{1,0:T(4,128)}, f32[4,128]{1,0:T(4,128)S(1)}, u32[]{:S(2)}, u32[]{:S(2)}) %collective-permute-start.6) | collective-permute-done | bytes 2080 | tf_op jit(solution)/shard_map/ppermute | solution.py:18
  48.7 5.9 %tick.6 = (f32[4,4,16,8,128]{4,3,2,1,0:T(8,128)}, f32[4,128]{1,0:T(4,128)}) custom-call(s32[1]{0:T(128)} %bitcast.start_ref, bf16[2,512,512]{2,1,0:T(8,128)(2,1)} %subtract_convert_fusion.dx_ref, bf16[2,128,512]{2,1,0:T(8,128)(2,1)} %copy-done.3, f32[4,128]{1,0:T(4,128)} %copy-done.8, f32[4,128]{1,0:T(4,128)} %before_ref.1, ...), custom_call_target="tpu_custom_call" | custom-call | tf_op jit(solution)/shard_map/tick/pallas_call | solution.py:155
  54.6 3.3 %collective-permute-start.7 = (f32[4,128]{1,0:T(4,128)}, f32[4,128]{1,0:T(4,128)S(1)}, u32[]{:S(2)}, u32[]{:S(2)}) collective-permute-start(f32[4,128]{1,0:T(4,128)} %get-tuple-element.16), channel_id=1, source_target_pairs={{0,4},{4,8},{8,12},{12,16},{16,20},{20,24},{24,28},{1,5},{5,9},{9,... | collective-permute-start | bytes 6152 | tf_op jit(solution)/shard_map/ppermute | solution.py:18
  58.6 2.5 %collective-permute-done.7.bottom_ref.before_ref = f32[4,128]{1,0:T(4,128)S(1)} collective-permute-done((f32[4,128]{1,0:T(4,128)}, f32[4,128]{1,0:T(4,128)S(1)}, u32[]{:S(2)}, u32[]{:S(2)}) %collective-permute-start.7) | collective-permute-done | bytes 2080 | tf_op jit(solution)/shard_map/ppermute | solution.py:18
  61.7 5.8 %tick.7 = (f32[4,4,16,8,128]{4,3,2,1,0:T(8,128)}, f32[4,128]{1,0:T(4,128)}) custom-call(s32[1]{0:T(128)} %bitcast.start_ref, bf16[2,512,512]{2,1,0:T(8,128)(2,1)} %subtract_convert_fusion.dx_ref, bf16[2,128,512]{2,1,0:T(8,128)(2,1)} %copy-done.2, f32[4,128]{1,0:T(4,128)} %copy-done.5, f32[4,128]{1,0:T(4,128)} %copy-done.8, ...), custom_call_target="tpu_custom_call" | custom-call | tf_op jit(solution)/shard_map/tick/pallas_call | solution.py:155
  67.5 2.4 %collective-permute-start.8 = (f32[4,128]{1,0:T(4,128)}, f32[4,128]{1,0:T(4,128)S(1)}, u32[]{:S(2)}, u32[]{:S(2)}) collective-permute-start(f32[4,128]{1,0:T(4,128)} %get-tuple-element.18), channel_id=1, source_target_pairs={{0,4},{4,8},{8,12},{12,16},{16,20},{20,24},{24,28},{1,5},{5,9},{9,... | collective-permute-start | bytes 6152 | tf_op jit(solution)/shard_map/ppermute | solution.py:18
  70.9 3.2 %collective-permute-done.8.bottom_ref.before_ref = f32[4,128]{1,0:T(4,128)S(1)} collective-permute-done((f32[4,128]{1,0:T(4,128)}, f32[4,128]{1,0:T(4,128)S(1)}, u32[]{:S(2)}, u32[]{:S(2)}) %collective-permute-start.8) | collective-permute-done | bytes 2080 | tf_op jit(solution)/shard_map/ppermute | solution.py:18
  74.7 5.9 %tick.8 = (f32[4,4,16,8,128]{4,3,2,1,0:T(8,128)}, f32[4,128]{1,0:T(4,128)}) custom-call(s32[1]{0:T(128)} %bitcast.start_ref, bf16[2,512,512]{2,1,0:T(8,128)(2,1)} %subtract_convert_fusion.dx_ref, bf16[2,128,512]{2,1,0:T(8,128)(2,1)} %copy-done, f32[4,128]{1,0:T(4,128)} %copy-done.6, f32[4,128]{1,0:T(4,128)} %copy-done.5, ...), custom_call_target="tpu_custom_call" | custom-call | tf_op jit(solution)/shard_map/tick/pallas_call | solution.py:155
  80.6 1.9 %collective-permute-start.9 = (f32[4,128]{1,0:T(4,128)}, f32[4,128]{1,0:T(4,128)S(1)}, u32[]{:S(2)}, u32[]{:S(2)}) collective-permute-start(f32[4,128]{1,0:T(4,128)} %get-tuple-element.20), channel_id=1, source_target_pairs={{0,4},{4,8},{8,12},{12,16},{16,20},{20,24},{24,28},{1,5},{5,9},{9,... | collective-permute-start | bytes 6152 | tf_op jit(solution)/shard_map/ppermute | solution.py:18
  83.2 4.0 %collective-permute-done.9.bottom_ref.before_ref = f32[4,128]{1,0:T(4,128)S(1)} collective-permute-done((f32[4,128]{1,0:T(4,128)}, f32[4,128]{1,0:T(4,128)S(1)}, u32[]{:S(2)}, u32[]{:S(2)}) %collective-permute-start.9) | collective-permute-done | bytes 2080 | tf_op jit(solution)/shard_map/ppermute | solution.py:18
  87.7 5.8 %tick.9 = (f32[4,4,16,8,128]{4,3,2,1,0:T(8,128)}, f32[4,128]{1,0:T(4,128)}) custom-call(s32[1]{0:T(128)} %bitcast.start_ref, bf16[2,512,512]{2,1,0:T(8,128)(2,1)} %subtract_convert_fusion.dx_ref, bf16[2,128,512]{2,1,0:T(8,128)(2,1)} %copy-done.1, f32[4,128]{1,0:T(4,128)} %copy-done.7, f32[4,128]{1,0:T(4,128)} %copy-done.6, ...), custom_call_target="tpu_custom_call" | custom-call | tf_op jit(solution)/shard_map/tick/pallas_call | solution.py:155
  93.6 1.9 %collective-permute-start.10 = (f32[4,128]{1,0:T(4,128)}, f32[4,128]{1,0:T(4,128)S(1)}, u32[]{:S(2)}, u32[]{:S(2)}) collective-permute-start(f32[4,128]{1,0:T(4,128)} %get-tuple-element.22), channel_id=1, source_target_pairs={{0,4},{4,8},{8,12},{12,16},{16,20},{20,24},{24,28},{1,5},{5,9},{9,... | collective-permute-start | bytes 6152 | tf_op jit(solution)/shard_map/ppermute | solution.py:18
  96.2 4.0 %collective-permute-done.10.bottom_ref = f32[4,128]{1,0:T(4,128)S(1)} collective-permute-done((f32[4,128]{1,0:T(4,128)}, f32[4,128]{1,0:T(4,128)S(1)}, u32[]{:S(2)}, u32[]{:S(2)}) %collective-permute-start.10) | collective-permute-done | bytes 2080 | tf_op jit(solution)/shard_map/ppermute | solution.py:18
  100.9 5.5 %tick_last.1 = (f32[4,512]{1,0:T(4,128)}, f32[4,128]{1,0:T(4,128)}) custom-call(s32[1]{0:T(128)} %bitcast.start_ref, bf16[2,512,512]{2,1,0:T(8,128)(2,1)} %subtract_convert_fusion.dx_ref, bf16[2,128,512]{2,1,0:T(8,128)(2,1)} %copy-done.4, f32[4,128]{1,0:T(4,128)} %copy-done.9, f32[4,128]{1,0:T(4,128)} %copy-done.7, ...), custom_call_target="tpu_custom_call" | custom-call | tf_op jit(solution)/shard_map/tick_last/pallas_call | solution.py:155
  (41 shorter events, 11.7 us)
Async XLA Ops:
  0.6 9.2 %collective-permute-start.1 = (bf16[2,128,512]{2,1,0:T(8,128)(2,1)}, bf16[2,128,512]{2,1,0:T(8,128)(2,1)S(1)}, u32[]{:S(2)}, u32[]{:S(2)}) collective-permute-start(bf16[2,128,512]{2,1,0:T(8,128)(2,1)} %y_ref.1), channel_id=1, source_target_pairs={{0,4},{4,8},{8,12},{12,16},{16,20},{20,24},{24,28},{28,0},{1,5},{5... | collective-permute-start | bytes 786440 | tf_op jit(solution)/shard_map/ppermute | solution.py:23
  9.8 23.8 %copy-start.3 = (bf16[2,128,512]{2,1,0:T(8,128)(2,1)}, bf16[2,128,512]{2,1,0:T(8,128)(2,1)S(1)}, u32[]{:S(2)}) copy-start(bf16[2,128,512]{2,1,0:T(8,128)(2,1)S(1)} %collective-permute-done.1.y_ref) | copy-start | bytes 786436
  9.8 8.1 %collective-permute-start.2 = (bf16[2,128,512]{2,1,0:T(8,128)(2,1)S(1)}, bf16[2,128,512]{2,1,0:T(8,128)(2,1)S(1)}, u32[]{:S(2)}, u32[]{:S(2)}) collective-permute-start(bf16[2,128,512]{2,1,0:T(8,128)(2,1)S(1)} %collective-permute-done.1.y_ref), channel_id=1, source_target_pairs={{0,4},{4,8},{8,12},{12,16},{16,20},{20,24},{24,28},{28,0},{1,5},{5... | collective-permute-start | bytes 786440 | tf_op jit(solution)/shard_map/ppermute | solution.py:23
  17.9 15.8 %copy-start.2 = (bf16[2,128,512]{2,1,0:T(8,128)(2,1)}, bf16[2,128,512]{2,1,0:T(8,128)(2,1)S(1)}, u32[]{:S(2)}) copy-start(bf16[2,128,512]{2,1,0:T(8,128)(2,1)S(1)} %collective-permute-done.2.y_ref) | copy-start | bytes 786436
  17.9 10.3 %collective-permute-start.3 = (bf16[2,128,512]{2,1,0:T(8,128)(2,1)S(1)}, bf16[2,128,512]{2,1,0:T(8,128)(2,1)S(1)}, u32[]{:S(2)}, u32[]{:S(2)}) collective-permute-start(bf16[2,128,512]{2,1,0:T(8,128)(2,1)S(1)} %collective-permute-done.2.y_ref), channel_id=1, source_target_pairs={{0,4},{4,8},{8,12},{12,16},{16,20},{20,24},{24,28},{28,0},{1,5},{5... | collective-permute-start | bytes 786440 | tf_op jit(solution)/shard_map/ppermute | solution.py:23
  19.2 8.4 %collective-permute-start = (bf16[2,1,512]{2,1,0:T(2,128)(2,1)S(1)}, bf16[2,1,512]{2,1,0:T(2,128)(2,1)S(1)}, u32[]{:S(2)}, u32[]{:S(2)}) collective-permute-start(bf16[2,1,512]{2,1,0:T(2,128)(2,1)S(1)} %slice.6), channel_id=1, source_target_pairs={{0,4},{4,8},{8,12},{12,16},{16,20},{20,24},{24,28},{1,5},{5,9},{9,... | collective-permute-start | bytes 6152 | tf_op jit(solution)/shard_map/ppermute | solution.py:18
  28.3 5.4 %copy-start = (bf16[2,128,512]{2,1,0:T(8,128)(2,1)}, bf16[2,128,512]{2,1,0:T(8,128)(2,1)S(1)}, u32[]{:S(2)}) copy-start(bf16[2,128,512]{2,1,0:T(8,128)(2,1)S(1)} %collective-permute-done.3.y_ref) | copy-start | bytes 786436
  28.3 41.7 %collective-permute-start.4 = (bf16[2,128,512]{2,1,0:T(8,128)(2,1)S(1)}, bf16[2,128,512]{2,1,0:T(8,128)(2,1)S(1)}, u32[]{:S(2)}, u32[]{:S(2)}) collective-permute-start(bf16[2,128,512]{2,1,0:T(8,128)(2,1)S(1)} %collective-permute-done.3.y_ref), channel_id=1, source_target_pairs={{0,4},{4,8},{8,12},{12,16},{16,20},{20,24},{24,28},{28,0},{1,5},{5... | collective-permute-start | bytes 786440 | tf_op jit(solution)/shard_map/ppermute | solution.py:23
  33.7 1.3 %copy-start.10 = (f32[4,1]{0,1:T(1,128)S(1)}, f32[4,1]{0,1:T(1,128)}, u32[]{:S(2)}) copy-start(f32[4,1]{0,1:T(1,128)} %param.11) | copy-start | bytes 52
  41.5 6.6 %collective-permute-start.6 = (f32[4,128]{1,0:T(4,128)}, f32[4,128]{1,0:T(4,128)S(1)}, u32[]{:S(2)}, u32[]{:S(2)}) collective-permute-start(f32[4,128]{1,0:T(4,128)} %get-tuple-element.14), channel_id=1, source_target_pairs={{0,4},{4,8},{8,12},{12,16},{16,20},{20,24},{24,28},{1,5},{5,9},{9,... | collective-permute-start | bytes 6152 | tf_op jit(solution)/shard_map/ppermute | solution.py:18
  48.1 0.6 copy-start.8
  54.6 6.6 %collective-permute-start.7 = (f32[4,128]{1,0:T(4,128)}, f32[4,128]{1,0:T(4,128)S(1)}, u32[]{:S(2)}, u32[]{:S(2)}) collective-permute-start(f32[4,128]{1,0:T(4,128)} %get-tuple-element.16), channel_id=1, source_target_pairs={{0,4},{4,8},{8,12},{12,16},{16,20},{20,24},{24,28},{1,5},{5,9},{9,... | collective-permute-start | bytes 6152 | tf_op jit(solution)/shard_map/ppermute | solution.py:18
  61.1 0.6 copy-start.5
  67.5 6.6 %collective-permute-start.8 = (f32[4,128]{1,0:T(4,128)}, f32[4,128]{1,0:T(4,128)S(1)}, u32[]{:S(2)}, u32[]{:S(2)}) collective-permute-start(f32[4,128]{1,0:T(4,128)} %get-tuple-element.18), channel_id=1, source_target_pairs={{0,4},{4,8},{8,12},{12,16},{16,20},{20,24},{24,28},{1,5},{5,9},{9,... | collective-permute-start | bytes 6152 | tf_op jit(solution)/shard_map/ppermute | solution.py:18
  70.0 10.6 %copy-start.1 = (bf16[2,128,512]{2,1,0:T(8,128)(2,1)}, bf16[2,128,512]{2,1,0:T(8,128)(2,1)S(1)}, u32[]{:S(2)}) copy-start(bf16[2,128,512]{2,1,0:T(8,128)(2,1)S(1)} %collective-permute-done.4.y_ref) | copy-start | bytes 786436
  70.0 30.1 %collective-permute-start.5 = (bf16[2,128,512]{2,1,0:T(8,128)(2,1)S(1)}, bf16[2,128,512]{2,1,0:T(8,128)(2,1)S(1)}, u32[]{:S(2)}, u32[]{:S(2)}) collective-permute-start(bf16[2,128,512]{2,1,0:T(8,128)(2,1)S(1)} %collective-permute-done.4.y_ref), channel_id=1, source_target_pairs={{0,4},{4,8},{8,12},{12,16},{16,20},{20,24},{24,28},{28,0},{1,5},{5... | collective-permute-start | bytes 786440 | tf_op jit(solution)/shard_map/ppermute | solution.py:23
  74.1 0.6 copy-start.6
  80.6 6.6 %collective-permute-start.9 = (f32[4,128]{1,0:T(4,128)}, f32[4,128]{1,0:T(4,128)S(1)}, u32[]{:S(2)}, u32[]{:S(2)}) collective-permute-start(f32[4,128]{1,0:T(4,128)} %get-tuple-element.20), channel_id=1, source_target_pairs={{0,4},{4,8},{8,12},{12,16},{16,20},{20,24},{24,28},{1,5},{5,9},{9,... | collective-permute-start | bytes 6152 | tf_op jit(solution)/shard_map/ppermute | solution.py:18
  87.1 0.6 copy-start.7
  93.6 6.6 %collective-permute-start.10 = (f32[4,128]{1,0:T(4,128)}, f32[4,128]{1,0:T(4,128)S(1)}, u32[]{:S(2)}, u32[]{:S(2)}) collective-permute-start(f32[4,128]{1,0:T(4,128)} %get-tuple-element.22), channel_id=1, source_target_pairs={{0,4},{4,8},{8,12},{12,16},{16,20},{20,24},{24,28},{1,5},{5,9},{9,... | collective-permute-start | bytes 6152 | tf_op jit(solution)/shard_map/ppermute | solution.py:18
  100.2 0.6 copy-start.9
  100.2 0.7 copy-start.4
  107.1 0.6 copy-start.11
where the time goes:
time: 108 us
  Pallas kernels  34.8 us (32%)
  waiting for transfers between devices  30.8 us (29%)
  starting transfers between devices  26.2 us (24%)
  local copies, waits for them, and re-layouts  11.3 us (10%)
  other arithmetic  3.77 us (3%)
    pallas_call x6, Pallas kernels, tick(): pl.pallas_call(functools.partial(tick_kernel, last), out_shape=(left_out,...  34.8 us
    ppermute x6, starting transfers between devices, shifted(): return lax.ppermute(x, axis, pairs)  20.9 us
    ppermute x6, waiting for transfers between devices, shifted(): return lax.ppermute(x, axis, pairs)  15.7 us
    ppermute x5, waiting for transfers between devices, passed_along(): return lax.ppermute(x, axis, [(i, (i + by) % count) for i in range(count)])  15.1 us
    unnamed x29, local copies, waits for them, and re-layouts  7.08 us
    ppermute x5, starting transfers between devices, passed_along(): return lax.ppermute(x, axis, [(i, (i + by) % count) for i in range(count)])  5.27 us
    convert_element_type x1, other arithmetic, local(): (x_path.astype(jnp.float32) - earlier.astype(jnp.float32)).astype(jnp.bfl...  3.08 us
  transfers between devices with their start and end apart: 11, of which 8 were waited for; matrix products, arithmetic and copies ran while one was open for 10% of the time, Pallas kernels for 27%

commit v1 on v0

--- a/solution.py
+++ b/solution.py
@@ -7,9 +7,11 @@
 from jax.experimental.pallas import tpu as pltpu
 from jax.sharding import PartitionSpec as P
 
+
 TICKS = 6
 PASSES = 4
 SUB = 8
+VMEM_BYTES = 16 * 1024 * 1024
 
 
 def shifted(x, axis, by):
@@ -29,15 +31,53 @@
     return jnp.concatenate([high, low], axis=1)
 
 
-def tick_kernel(
-    last, start_ref, dx_ref, y_ref, bottom_ref, before_ref, left_ref, out_ref, top_ref, products_ref
-):
+def prep_kernel(x_ref, anchor_ref, left_ref, dx_ref, edge_ref, head_ref):
+    series_x, _, _ = x_ref.shape
+    pairs, levels, groups, _, tile = edge_ref.shape
+    for m in range(series_x):
+        x = x_ref[m].astype(jnp.float32)
+        head_ref[m] = x[0:SUB]
+        first = lax.broadcasted_iota(jnp.int32, x.shape, 0) == 0
+        anchor = jnp.broadcast_to(anchor_ref[m : m + 1, :].astype(jnp.float32), x.shape)
+        dx_ref[m] = (x - jnp.where(first, anchor, pltpu.roll(x, 1, 0))).astype(jnp.bfloat16)
+    sub = lax.broadcasted_iota(jnp.int32, (SUB, tile), 0)
+    lane = lax.broadcasted_iota(jnp.int32, (SUB, tile), 1)
+    for p in range(pairs):
+        for r in range(levels):
+            row = jnp.broadcast_to(left_ref[p : p + 1, r * tile : (r + 1) * tile], (SUB, tile))
+            for j in range(groups):
+                own = jnp.where(lane == sub * groups + j, row, 0.0)
+                edge_ref[p, r, j] = jnp.broadcast_to(
+                    jnp.sum(own, axis=1, keepdims=True), (SUB, tile)
+                )
+
+
+def tick_kernel(at, last, *refs):
+    start_ref, dx_ref, y_ref, bottom_ref, before_ref, left_ref, *refs = refs
+    if at == 0:
+        head_ref, received_ref, *refs = refs
+    else:
+        row_ref, *refs = refs
+    earlier_refs = []
+    if last:
+        earlier_refs, refs = refs[:at], refs[at:]
+    out_ref, top_ref, *refs = refs
+    if not last:
+        after_ref, *refs = refs
+    if at == 0:
+        row_ref, *refs = refs
+    (products_ref,) = refs
     series_x, block_len, channels = dx_ref.shape
     series_y, tile, _ = y_ref.shape
     pairs = series_x * series_y
     levels = block_len // tile
     groups = tile // SUB
-
+    at_start = start_ref[0] == 1
+
+    if at == 0:
+        for m in range(series_x):
+            jump = head_ref[m] - received_ref[m].astype(jnp.float32)
+            row_ref[m] = jnp.where(at_start, dx_ref[m, 0:SUB, :].astype(jnp.float32), jump)
     y_all = y_ref[...].reshape(series_y * tile, channels)
     for m in range(series_x):
         both = lax.dot_general(
@@ -45,6 +85,14 @@
         )
         for n in range(series_y):
             products_ref[m * series_y + n] = both[:, n * tile : (n + 1) * tile]
+        both = lax.dot_general(
+            row_ref[m].astype(jnp.bfloat16),
+            y_all,
+            (((1,), (1,)), ((), ())),
+            preferred_element_type=jnp.float32,
+        )
+        for n in range(series_y):
+            products_ref[m * series_y + n, 0:1, :] = both[0:1, n * tile : (n + 1) * tile]
 
     row = lax.broadcasted_iota(jnp.int32, (2 * tile, tile), 0) % tile
     col = lax.broadcasted_iota(jnp.int32, (2 * tile, tile), 1)
@@ -54,7 +102,6 @@
     edge_sums = jnp.concatenate([strict, inclusive], axis=1)
     sub = lax.broadcasted_iota(jnp.int32, (SUB, tile), 0)
     lane = lax.broadcasted_iota(jnp.int32, (SUB, tile), 1)
-    at_start = start_ref[0] == 1
 
     def sum_before(total):
         out = jnp.where(sub >= 1, pltpu.roll(total, 1, 0), 0.0)
@@ -82,6 +129,8 @@
         c = jnp.where(at_start, 1.0, c)
         bottom.append(b)
         corner.append(c)
+        if not last:
+            after_ref[p : p + 1, :] = b[0:1]
         bottom_shift.append(jnp.where(lane == 0, c, pltpu.roll(b, 1, 1)))
 
     for r in range(levels):
@@ -140,54 +189,83 @@
             bottom[p] = bottom[p] + lift + sums[:, tile:]
             bottom_shift[p] = bottom_shift[p] + lift + sums[:, :tile]
             corner[p] = end[p]
+    for k, earlier_ref in enumerate(earlier_refs):
+        top_ref[:, k * tile : (k + 1) * tile] = earlier_ref[...]
+    begin = len(earlier_refs) * tile
     for p in range(pairs):
-        top_ref[p : p + 1, :] = bottom[p][0:1]
-
-
-def tick(start, dx, y, bottom, before, left, last):
+        top_ref[p : p + 1, begin : begin + tile] = bottom[p][0:1]
+
+
+VMEM = pl.BlockSpec(memory_space=pltpu.VMEM)
+
+
+def prepare(x_path, x_anchor, left_in, tile):
+    pairs, block_len = left_in.shape
+    edge = (pairs, block_len // tile, tile // SUB, SUB, tile)
+    return pl.pallas_call(
+        prep_kernel,
+        out_shape=(
+            jax.ShapeDtypeStruct(x_path.shape, jnp.bfloat16),
+            jax.ShapeDtypeStruct(edge, jnp.float32),
+            jax.ShapeDtypeStruct((x_path.shape[0], SUB, x_path.shape[2]), jnp.float32),
+        ),
+        in_specs=[VMEM] * 3,
+        out_specs=(VMEM, VMEM, VMEM),
+        compiler_params=pltpu.CompilerParams(vmem_limit_bytes=VMEM_BYTES),
+        name="prep",
+    )(x_path, x_anchor, left_in)
+
+
+def tick(at, last, start, dx, y, bottom, before, left, first, tops):
     pairs, tile = bottom.shape
-    block_len = dx.shape[1]
-    vmem = pl.BlockSpec(memory_space=pltpu.VMEM)
+    series_x, block_len, channels = dx.shape
+    edge = jax.ShapeDtypeStruct((pairs, tile), jnp.float32)
     if last:
-        left_out = jax.ShapeDtypeStruct((pairs, block_len), jnp.float32)
+        shapes = [
+            jax.ShapeDtypeStruct((pairs, block_len), jnp.float32),
+            jax.ShapeDtypeStruct((pairs, tile * (at + 1)), jnp.float32),
+        ]
+        first = first + tops
     else:
-        left_out = jax.ShapeDtypeStruct(left.shape, jnp.float32)
+        shapes = [jax.ShapeDtypeStruct(left.shape, jnp.float32), edge, edge]
+    if at == 0:
+        shapes.append(jax.ShapeDtypeStruct((series_x, SUB, channels), jnp.float32))
+    specs = [pl.BlockSpec(memory_space=pltpu.SMEM)] + [VMEM] * (5 + len(first))
     return pl.pallas_call(
-        functools.partial(tick_kernel, last),
-        out_shape=(left_out, jax.ShapeDtypeStruct((pairs, tile), jnp.float32)),
-        in_specs=[pl.BlockSpec(memory_space=pltpu.SMEM)] + [vmem] * 5,
-        out_specs=(vmem, vmem),
+        functools.partial(tick_kernel, at, last),
+        out_shape=tuple(shapes),
+        in_specs=specs,
+        out_specs=(VMEM,) * len(shapes),
         scratch_shapes=[pltpu.VMEM((pairs, block_len, tile), jnp.float32)],
-        name="tick_last" if last else "tick",
-    )(start, dx, y, bottom, before, left)
+        compiler_params=pltpu.CompilerParams(vmem_limit_bytes=VMEM_BYTES),
+        name="tick",
+    )(start, dx, y, bottom, before, left, *first)
 
 
 def local(x_path, x_anchor, y_steps, left_in, bottom_in, corner_in):
-    series_x, block_len, channels = x_path.shape
-    series_y, tile, _ = y_steps.shape
-    pairs = series_x * series_y
-    levels = block_len // tile
-    groups = tile // SUB
+    tile = y_steps.shape[1]
     at_start = lax.axis_index("tm") == 0
     start = at_start.astype(jnp.int32).reshape(1)
     received = shifted(x_path[:, -1:, :], "tm", 1)
-    before = jnp.where(at_start, x_anchor[:, None, :], received)
-    earlier = jnp.concatenate([before, x_path[:, :-1, :]], axis=1)
-    dx = (x_path.astype(jnp.float32) - earlier.astype(jnp.float32)).astype(jnp.bfloat16)
-    left = left_in.reshape(pairs, levels, SUB, groups).transpose(0, 1, 3, 2)
-    left = jnp.broadcast_to(left[..., None], left.shape + (tile,))
-    bottom = bottom_in
-    previous = jnp.broadcast_to(corner_in, (pairs, tile))
-    y_now = y_steps
-    tops = []
+    y_next = passed_along(y_steps, "tm", 1)
+    dx, left, head = prepare(x_path, x_anchor, left_in, tile)
+    y_now, bottom = y_steps, bottom_in
+    previous = jnp.broadcast_to(corner_in, bottom_in.shape)
+    first, tops = [head, received], []
     for t in range(TICKS):
-        y_next = passed_along(y_now, "tm", 1) if t < TICKS - 1 else None
-        left, top = tick(start, dx, y_now, bottom, previous, left, t == TICKS - 1)
+        last = t == TICKS - 1
+        left, top, *rest = tick(t, last, start, dx, y_now, bottom, previous, left, first, tops)
+        if last:
+            return left, top
         tops.append(top)
-        if t < TICKS - 1:
-            previous, bottom = bottom, shifted(top, "tm", 1)
-            y_now = y_next
-    return left, jnp.concatenate(tops, axis=1)
+        previous = rest[0]
+        if t == 0:
+            first = [rest[1]]
+        bottom = shifted(top, "tm", 1)
+        y_now = y_next
+        if t + 2 < TICKS:
+            y_now, _ = lax.optimization_barrier((y_now, top))
+            y_next = passed_along(y_now, "tm", 1)
 
 
 def solution(mesh):

time: 108 us -> 69.4 us (0.64)
  Pallas kernels: 34.8 us -> 22.3 us
  starting transfers between devices: 26.2 us -> 15.6 us
  local copies, waits for them, and re-layouts: 11.3 us -> 3.3 us
  waiting for transfers between devices: 30.8 us -> 26.6 us
  other arithmetic: 3.77 us -> 0 us
    ppermute x5, waiting for transfers between devices: 15.1 us -> 0.01 us  [passed_along(): return lax.ppermute(x, axis, [(i, (i + by) % count) for i in range(count)])]
    pallas_call x6 -> x7, Pallas kernels: 34.8 us -> 22.3 us  [the longest x6 21.4 us: tick(): pl.pallas_call(functools.partial(tick_kernel, at, last), out_shape=tuple(...]
    ppermute x6, waiting for transfers between devices: 15.7 us -> 26.6 us  [shifted(): return lax.ppermute(x, axis, pairs)]
    ppermute x6, starting transfers between devices: 20.9 us -> 13.2 us  [shifted(): return lax.ppermute(x, axis, pairs)]
    unnamed x29 -> x12, local copies, waits for them, and re-layouts: 7.08 us -> 2.51 us
    convert_element_type x1 -> x0, other arithmetic: 3.08 us -> none  [local(): (x_path.astype(jnp.float32) - earlier.astype(jnp.float32)).astype(jnp.bfl...]
    ppermute x5, starting transfers between devices: 5.27 us -> 2.42 us  [passed_along(): return lax.ppermute(x, axis, [(i, (i + by) % count) for i in range(count)])]
    broadcast_in_dim x2 -> x1, local copies, waits for them, and re-layouts: 1.97 us -> 0.07 us  [local(): previous = jnp.broadcast_to(corner_in, bottom_in.shape)]
  transfers between devices with their start and end apart: 11 -> 11, of which waited for: 8 -> 6; matrix products, arithmetic and copies ran while one was open for 10% -> 1% of each run, Pallas kernels for 27% -> 27%
where the time goes in v1:
time: 69.4 us; the launch traced here: 68.7 us
  waiting for transfers between devices  26.6 us (38%)
  Pallas kernels  22.3 us (32%)
  starting transfers between devices  15.6 us (22%)
  local copies, waits for them, and re-layouts  3.3 us (5%)
  between operations  0.8 us (1%)
    ppermute x6, waiting for transfers between devices, shifted(): return lax.ppermute(x, axis, pairs)  26.6 us
    pallas_call x6, Pallas kernels, tick(): pl.pallas_call(functools.partial(tick_kernel, at, last), out_shape=tuple(...  21.4 us
    ppermute x6, starting transfers between devices, shifted(): return lax.ppermute(x, axis, pairs)  13.2 us
    unnamed x12, local copies, waits for them, and re-layouts  2.51 us
    ppermute x5, starting transfers between devices, passed_along(): return lax.ppermute(x, axis, [(i, (i + by) % count) for i in range(count)])  2.42 us
  transfers between devices with their start and end apart: 11, of which 6 were waited for; matrix products, arithmetic and copies ran while one was open for 1% of the time, Pallas kernels for 27%

profile of v1, /device:TPU:24, one launch (start us, length us, event | category | flops | bytes accessed | tf_op | source)
XLA Modules:
  0.0 68.7 jit_solution(9264796038647948876)
XLA Ops:
  0.6 1.6 %collective-permute-start = (bf16[2,128,512]{2,1,0:T(8,128)(2,1)}, bf16[2,128,512]{2,1,0:T(8,128)(2,1)S(1)}, u32[]{:S(2)}, u32[]{:S(2)}) collective-permute-start(bf16[2,128,512]{2,1,0:T(8,128)(2,1)} %refs_2_.1), channel_id=1, source_target_pairs={{0,4},{4,8},{8,12},{12,16},{16,20},{20,24},{24,28},{28,0},{1,5},{5... | collective-permute-start | bytes 786440 | tf_op jit(solution)/shard_map/ppermute | solution.py:25
  2.2 0.7 %slice.3 = bf16[2,1,512]{2,1,0:T(2,128)(2,1)S(1)} slice(bf16[2,512,512]{2,1,0:T(8,128)(2,1)} %x_ref.1), slice={[0:2], [511:512], [0:512]} | slice | bytes 4096 | tf_op jit(solution)/shard_map/slice | solution.py:249
  2.9 1.9 %collective-permute-start.1 = (bf16[2,1,512]{2,1,0:T(2,128)(2,1)S(1)}, bf16[2,1,512]{2,1,0:T(2,128)(2,1)S(1)}, u32[]{:S(2)}, u32[]{:S(2)}) collective-permute-start(bf16[2,1,512]{2,1,0:T(2,128)(2,1)S(1)} %slice.3), channel_id=1, source_target_pairs={{0,4},{4,8},{8,12},{12,16},{16,20},{20,24},{24,28},{1,5},{5,9},{9,... | collective-permute-start | bytes 6152 | tf_op jit(solution)/shard_map/ppermute | solution.py:20
  4.9 0.7 copy-done.3
  5.6 1.2 %copy-done = bf16[2,512,512]{2,1,0:T(8,128)(2,1)S(1)} copy-done((bf16[2,512,512]{2,1,0:T(8,128)(2,1)S(1)}, bf16[2,512,512]{2,1,0:T(8,128)(2,1)}, u32[]{:S(2)}) %copy-start) | copy-done | bytes 1048600
  6.8 0.9 %prep.1 = (bf16[2,512,512]{2,1,0:T(8,128)(2,1)S(1)}, f32[4,4,16,8,128]{4,3,2,1,0:T(8,128)S(1)}, f32[2,8,512]{2,1,0:T(8,128)S(1)}) custom-call(bf16[2,512,512]{2,1,0:T(8,128)(2,1)S(1)} %copy-done, bf16[2,512]{1,0:T(2,128)(2,1)S(1)} %copy-done.3, f32[4,512]{1,0:T(4,128)S(1)} %copy-done.2), custom_call_target="tpu_custom_call" | custom-call | tf_op jit(solution)/shard_map/prep/pallas_call | solution.py:205
  7.7 2.2 %collective-permute-done.1.refs_7_ = bf16[2,1,512]{2,1,0:T(2,128)(2,1)S(1)} collective-permute-done((bf16[2,1,512]{2,1,0:T(2,128)(2,1)S(1)}, bf16[2,1,512]{2,1,0:T(2,128)(2,1)S(1)}, u32[]{:S(2)}, u32[]{:S(2)}) %collective-permute-start.1) | collective-permute-done | bytes 2080 | tf_op jit(solution)/shard_map/ppermute | solution.py:20
  10.6 3.5 %tick.6 = (f32[4,4,16,8,128]{4,3,2,1,0:T(8,128)S(1)}, f32[4,128]{1,0:T(4,128)S(1)}, f32[4,128]{1,0:T(4,128)S(1)}, f32[2,8,512]{2,1,0:T(8,128)S(1)}) custom-call(s32[1]{0:T(128)} %bitcast.refs_0_, bf16[2,512,512]{2,1,0:T(8,128)(2,1)S(1)} %get-tuple-element.25.refs_1_, bf16[2,128,512]{2,1,0:T(8,128)(2,1)S(1)} %copy-done.1, f32[4,128]{1,0:T(4,128)S(1)} %copy-done.4, ...), custom_call_target="tpu_custom_call" | custom-call | tf_op jit(solution)/shard_map/tick/pallas_call | solution.py:234
  14.1 0.7 collective-permute-start.2
  14.8 2.3 %collective-permute-start.3 = (f32[4,128]{1,0:T(4,128)S(1)}, f32[4,128]{1,0:T(4,128)S(1)}, u32[]{:S(2)}, u32[]{:S(2)}) collective-permute-start(f32[4,128]{1,0:T(4,128)S(1)} %get-tuple-element.28.refs_7_), channel_id=1, source_target_pairs={{0,4},{4,8},{8,12},{12,16},{16,20},{20,24},{24,28},{1,5},{5,9},{9,... | collective-permute-start | bytes 6152 | tf_op jit(solution)/shard_map/ppermute | solution.py:20
  17.0 5.2 %collective-permute-done.3.refs_3_ = f32[4,128]{1,0:T(4,128)S(1)} collective-permute-done((f32[4,128]{1,0:T(4,128)S(1)}, f32[4,128]{1,0:T(4,128)S(1)}, u32[]{:S(2)}, u32[]{:S(2)}) %collective-permute-start.3) | collective-permute-done | bytes 2080 | tf_op jit(solution)/shard_map/ppermute | solution.py:20
  22.3 3.4 %tick.7 = (f32[4,4,16,8,128]{4,3,2,1,0:T(8,128)S(1)}, f32[4,128]{1,0:T(4,128)S(1)}, f32[4,128]{1,0:T(4,128)S(1)}) custom-call(s32[1]{0:T(128)} %bitcast.refs_0_, bf16[2,512,512]{2,1,0:T(8,128)(2,1)S(1)} %get-tuple-element.25.refs_1_, bf16[2,128,512]{2,1,0:T(8,128)(2,1)S(1)} %collective-permute-done.refs_2_, f32[4,128]{1,0:T(4,128)S(1)} %collective-permute-done.3.refs_3_, ...), custom_call_target="tpu_custom_call" | custom-call | tf_op jit(solution)/shard_map/tick/pallas_call | solution.py:234
  25.8 1.9 %collective-permute-start.5 = (f32[4,128]{1,0:T(4,128)S(1)}, f32[4,128]{1,0:T(4,128)S(1)}, u32[]{:S(2)}, u32[]{:S(2)}) collective-permute-start(f32[4,128]{1,0:T(4,128)S(1)} %get-tuple-element.33.refs_8_), channel_id=1, source_target_pairs={{0,4},{4,8},{8,12},{12,16},{16,20},{20,24},{24,28},{1,5},{5,9},{9,... | collective-permute-start | bytes 6152 | tf_op jit(solution)/shard_map/ppermute | solution.py:20
  27.7 5.4 %collective-permute-done.5.refs_3_ = f32[4,128]{1,0:T(4,128)S(1)} collective-permute-done((f32[4,128]{1,0:T(4,128)S(1)}, f32[4,128]{1,0:T(4,128)S(1)}, u32[]{:S(2)}, u32[]{:S(2)}) %collective-permute-start.5) | collective-permute-done | bytes 2080 | tf_op jit(solution)/shard_map/ppermute | solution.py:20
  33.1 3.5 %tick.8 = (f32[4,4,16,8,128]{4,3,2,1,0:T(8,128)S(1)}, f32[4,128]{1,0:T(4,128)S(1)}, f32[4,128]{1,0:T(4,128)S(1)}) custom-call(s32[1]{0:T(128)} %bitcast.refs_0_, bf16[2,512,512]{2,1,0:T(8,128)(2,1)S(1)} %get-tuple-element.25.refs_1_, bf16[2,128,512]{2,1,0:T(8,128)(2,1)S(1)} %collective-permute-done.2.refs_2_, f32[4,128]{1,0:T(4,128)S(1)} %collective-permute-done.5.refs_3_, ...), custom_call_target="tpu_custom_call" | custom-call | tf_op jit(solution)/shard_map/tick/pallas_call | solution.py:234
  36.6 2.7 %collective-permute-start.7 = (f32[4,128]{1,0:T(4,128)S(1)}, f32[4,128]{1,0:T(4,128)S(1)}, u32[]{:S(2)}, u32[]{:S(2)}) collective-permute-start(f32[4,128]{1,0:T(4,128)S(1)} %get-tuple-element.37.refs_9_), channel_id=1, source_target_pairs={{0,4},{4,8},{8,12},{12,16},{16,20},{20,24},{24,28},{1,5},{5,9},{9,... | collective-permute-start | bytes 6152 | tf_op jit(solution)/shard_map/ppermute | solution.py:20
  39.3 4.6 %collective-permute-done.7.refs_3_ = f32[4,128]{1,0:T(4,128)S(1)} collective-permute-done((f32[4,128]{1,0:T(4,128)S(1)}, f32[4,128]{1,0:T(4,128)S(1)}, u32[]{:S(2)}, u32[]{:S(2)}) %collective-permute-start.7) | collective-permute-done | bytes 2080 | tf_op jit(solution)/shard_map/ppermute | solution.py:20
  43.9 3.4 %tick.9 = (f32[4,4,16,8,128]{4,3,2,1,0:T(8,128)S(1)}, f32[4,128]{1,0:T(4,128)S(1)}, f32[4,128]{1,0:T(4,128)S(1)}) custom-call(s32[1]{0:T(128)} %bitcast.refs_0_, bf16[2,512,512]{2,1,0:T(8,128)(2,1)S(1)} %get-tuple-element.25.refs_1_, bf16[2,128,512]{2,1,0:T(8,128)(2,1)S(1)} %collective-permute-done.4.refs_2_, f32[4,128]{1,0:T(4,128)S(1)} %collective-permute-done.7.refs_3_, ...), custom_call_target="tpu_custom_call" | custom-call | tf_op jit(solution)/shard_map/tick/pallas_call | solution.py:234
  47.4 2.5 %collective-permute-start.9 = (f32[4,128]{1,0:T(4,128)S(1)}, f32[4,128]{1,0:T(4,128)S(1)}, u32[]{:S(2)}, u32[]{:S(2)}) collective-permute-start(f32[4,128]{1,0:T(4,128)S(1)} %get-tuple-element.41.refs_10_), channel_id=1, source_target_pairs={{0,4},{4,8},{8,12},{12,16},{16,20},{20,24},{24,28},{1,5},{5,9},{9,... | collective-permute-start | bytes 6152 | tf_op jit(solution)/shard_map/ppermute | solution.py:20
  49.9 4.8 %collective-permute-done.9.refs_3_ = f32[4,128]{1,0:T(4,128)S(1)} collective-permute-done((f32[4,128]{1,0:T(4,128)S(1)}, f32[4,128]{1,0:T(4,128)S(1)}, u32[]{:S(2)}, u32[]{:S(2)}) %collective-permute-start.9) | collective-permute-done | bytes 2080 | tf_op jit(solution)/shard_map/ppermute | solution.py:20
  54.7 3.5 %tick.10 = (f32[4,4,16,8,128]{4,3,2,1,0:T(8,128)S(1)}, f32[4,128]{1,0:T(4,128)S(1)}, f32[4,128]{1,0:T(4,128)S(1)}) custom-call(s32[1]{0:T(128)} %bitcast.refs_0_, bf16[2,512,512]{2,1,0:T(8,128)(2,1)S(1)} %get-tuple-element.25.refs_1_, bf16[2,128,512]{2,1,0:T(8,128)(2,1)S(1)} %collective-permute-done.6.refs_2_, f32[4,128]{1,0:T(4,128)S(1)} %collective-permute-done.9.refs_3_, ...), custom_call_target="tpu_custom_call" | custom-call | tf_op jit(solution)/shard_map/tick/pallas_call | solution.py:234
  58.2 1.9 %collective-permute-start.10 = (f32[4,128]{1,0:T(4,128)S(1)}, f32[4,128]{1,0:T(4,128)S(1)}, u32[]{:S(2)}, u32[]{:S(2)}) collective-permute-start(f32[4,128]{1,0:T(4,128)S(1)} %get-tuple-element.45.refs_11_), channel_id=1, source_target_pairs={{0,4},{4,8},{8,12},{12,16},{16,20},{20,24},{24,28},{1,5},{5,9},{9,... | collective-permute-start | bytes 6152 | tf_op jit(solution)/shard_map/ppermute | solution.py:20
  60.1 4.4 %collective-permute-done.10.refs_3_ = f32[4,128]{1,0:T(4,128)S(1)} collective-permute-done((f32[4,128]{1,0:T(4,128)S(1)}, f32[4,128]{1,0:T(4,128)S(1)}, u32[]{:S(2)}, u32[]{:S(2)}) %collective-permute-start.10) | collective-permute-done | bytes 2080 | tf_op jit(solution)/shard_map/ppermute | solution.py:20
  64.6 4.1 %tick.11 = (f32[4,512]{1,0:T(4,128)}, f32[4,768]{1,0:T(4,128)}) custom-call(s32[1]{0:T(128)} %bitcast.refs_0_, bf16[2,512,512]{2,1,0:T(8,128)(2,1)S(1)} %get-tuple-element.25.refs_1_, bf16[2,128,512]{2,1,0:T(8,128)(2,1)S(1)} %collective-permute-done.8.refs_2_, f32[4,128]{1,0:T(4,128)S(1)} %collective-permute-done.10.refs_3_, ...), custom_call_target="tpu_custom_call" | custom-call | tf_op jit(solution)/shard_map/tick/pallas_call | solution.py:234
  (19 shorter events, 0.9 us)
Async XLA Ops:
  0.6 4.3 %copy-start.2 = (f32[4,512]{1,0:T(4,128)S(1)}, f32[4,512]{1,0:T(4,128)}, u32[]{:S(2)}) copy-start(f32[4,512]{1,0:T(4,128)} %left_ref.1) | copy-start | bytes 24580
  0.6 13.4 %collective-permute-start = (bf16[2,128,512]{2,1,0:T(8,128)(2,1)}, bf16[2,128,512]{2,1,0:T(8,128)(2,1)S(1)}, u32[]{:S(2)}, u32[]{:S(2)}) collective-permute-start(bf16[2,128,512]{2,1,0:T(8,128)(2,1)} %refs_2_.1), channel_id=1, source_target_pairs={{0,4},{4,8},{8,12},{12,16},{16,20},{20,24},{24,28},{28,0},{1,5},{5... | collective-permute-start | bytes 786440 | tf_op jit(solution)/shard_map/ppermute | solution.py:25
  2.9 7.0 %collective-permute-start.1 = (bf16[2,1,512]{2,1,0:T(2,128)(2,1)S(1)}, bf16[2,1,512]{2,1,0:T(2,128)(2,1)S(1)}, u32[]{:S(2)}, u32[]{:S(2)}) collective-permute-start(bf16[2,1,512]{2,1,0:T(2,128)(2,1)S(1)} %slice.3), channel_id=1, source_target_pairs={{0,4},{4,8},{8,12},{12,16},{16,20},{20,24},{24,28},{1,5},{5,9},{9,... | collective-permute-start | bytes 6152 | tf_op jit(solution)/shard_map/ppermute | solution.py:20
  4.9 0.7 copy-start.3
  5.5 1.2 %copy-start = (bf16[2,512,512]{2,1,0:T(8,128)(2,1)S(1)}, bf16[2,512,512]{2,1,0:T(8,128)(2,1)}, u32[]{:S(2)}) copy-start(bf16[2,512,512]{2,1,0:T(8,128)(2,1)} %x_ref.1) | copy-start | bytes 3145732
  6.8 3.2 %copy-start.5 = (f32[4,1]{0,1:T(1,128)S(1)}, f32[4,1]{0,1:T(1,128)}, u32[]{:S(2)}) copy-start(f32[4,1]{0,1:T(1,128)} %param.11) | copy-start | bytes 52
  6.8 3.2 %copy-start.1 = (bf16[2,128,512]{2,1,0:T(8,128)(2,1)S(1)}, bf16[2,128,512]{2,1,0:T(8,128)(2,1)}, u32[]{:S(2)}) copy-start(bf16[2,128,512]{2,1,0:T(8,128)(2,1)} %refs_2_.1) | copy-start | bytes 786436
  9.9 0.7 copy-start.4
  14.1 11.6 %collective-permute-start.2 = (bf16[2,128,512]{2,1,0:T(8,128)(2,1)S(1)}, bf16[2,128,512]{2,1,0:T(8,128)(2,1)S(1)}, u32[]{:S(2)}, u32[]{:S(2)}) collective-permute-start(bf16[2,128,512]{2,1,0:T(8,128)(2,1)S(1)} %collective-permute-done.refs_2_), channel_id=1, source_target_pairs={{0,4},{4,8},{8,12},{12,16},{16,20},{20,24},{24,28},{28,0},{1,5},{5... | collective-permute-start | bytes 786440 | tf_op jit(solution)/shard_map/ppermute | solution.py:25
  14.8 7.5 %collective-permute-start.3 = (f32[4,128]{1,0:T(4,128)S(1)}, f32[4,128]{1,0:T(4,128)S(1)}, u32[]{:S(2)}, u32[]{:S(2)}) collective-permute-start(f32[4,128]{1,0:T(4,128)S(1)} %get-tuple-element.28.refs_7_), channel_id=1, source_target_pairs={{0,4},{4,8},{8,12},{12,16},{16,20},{20,24},{24,28},{1,5},{5,9},{9,... | collective-permute-start | bytes 6152 | tf_op jit(solution)/shard_map/ppermute | solution.py:20
  25.7 10.8 %collective-permute-start.4 = (bf16[2,128,512]{2,1,0:T(8,128)(2,1)S(1)}, bf16[2,128,512]{2,1,0:T(8,128)(2,1)S(1)}, u32[]{:S(2)}, u32[]{:S(2)}) collective-permute-start(bf16[2,128,512]{2,1,0:T(8,128)(2,1)S(1)} %collective-permute-done.2.refs_2_), channel_id=1, source_target_pairs={{0,4},{4,8},{8,12},{12,16},{16,20},{20,24},{24,28},{28,0},{1,5},{5... | collective-permute-start | bytes 786440 | tf_op jit(solution)/shard_map/ppermute | solution.py:25
  25.8 7.3 %collective-permute-start.5 = (f32[4,128]{1,0:T(4,128)S(1)}, f32[4,128]{1,0:T(4,128)S(1)}, u32[]{:S(2)}, u32[]{:S(2)}) collective-permute-start(f32[4,128]{1,0:T(4,128)S(1)} %get-tuple-element.33.refs_8_), channel_id=1, source_target_pairs={{0,4},{4,8},{8,12},{12,16},{16,20},{20,24},{24,28},{1,5},{5,9},{9,... | collective-permute-start | bytes 6152 | tf_op jit(solution)/shard_map/ppermute | solution.py:20
  36.6 10.8 %collective-permute-start.6 = (bf16[2,128,512]{2,1,0:T(8,128)(2,1)S(1)}, bf16[2,128,512]{2,1,0:T(8,128)(2,1)S(1)}, u32[]{:S(2)}, u32[]{:S(2)}) collective-permute-start(bf16[2,128,512]{2,1,0:T(8,128)(2,1)S(1)} %collective-permute-done.4.refs_2_), channel_id=1, source_target_pairs={{0,4},{4,8},{8,12},{12,16},{16,20},{20,24},{24,28},{28,0},{1,5},{5... | collective-permute-start | bytes 786440 | tf_op jit(solution)/shard_map/ppermute | solution.py:25
  36.6 7.3 %collective-permute-start.7 = (f32[4,128]{1,0:T(4,128)S(1)}, f32[4,128]{1,0:T(4,128)S(1)}, u32[]{:S(2)}, u32[]{:S(2)}) collective-permute-start(f32[4,128]{1,0:T(4,128)S(1)} %get-tuple-element.37.refs_9_), channel_id=1, source_target_pairs={{0,4},{4,8},{8,12},{12,16},{16,20},{20,24},{24,28},{1,5},{5,9},{9,... | collective-permute-start | bytes 6152 | tf_op jit(solution)/shard_map/ppermute | solution.py:20
  47.4 17.2 %collective-permute-start.8 = (bf16[2,128,512]{2,1,0:T(8,128)(2,1)S(1)}, bf16[2,128,512]{2,1,0:T(8,128)(2,1)S(1)}, u32[]{:S(2)}, u32[]{:S(2)}) collective-permute-start(bf16[2,128,512]{2,1,0:T(8,128)(2,1)S(1)} %collective-permute-done.6.refs_2_), channel_id=1, source_target_pairs={{0,4},{4,8},{8,12},{12,16},{16,20},{20,24},{24,28},{28,0},{1,5},{5... | collective-permute-start | bytes 786440 | tf_op jit(solution)/shard_map/ppermute | solution.py:25
  47.4 7.3 %collective-permute-start.9 = (f32[4,128]{1,0:T(4,128)S(1)}, f32[4,128]{1,0:T(4,128)S(1)}, u32[]{:S(2)}, u32[]{:S(2)}) collective-permute-start(f32[4,128]{1,0:T(4,128)S(1)} %get-tuple-element.41.refs_10_), channel_id=1, source_target_pairs={{0,4},{4,8},{8,12},{12,16},{16,20},{20,24},{24,28},{1,5},{5,9},{9,... | collective-permute-start | bytes 6152 | tf_op jit(solution)/shard_map/ppermute | solution.py:20
  58.2 6.4 %collective-permute-start.10 = (f32[4,128]{1,0:T(4,128)S(1)}, f32[4,128]{1,0:T(4,128)S(1)}, u32[]{:S(2)}, u32[]{:S(2)}) collective-permute-start(f32[4,128]{1,0:T(4,128)S(1)} %get-tuple-element.45.refs_11_), channel_id=1, source_target_pairs={{0,4},{4,8},{8,12},{12,16},{16,20},{20,24},{24,28},{1,5},{5,9},{9,... | collective-permute-start | bytes 6152 | tf_op jit(solution)/shard_map/ppermute | solution.py:20

commit v2 on v1

--- a/solution.py
+++ b/solution.py
@@ -52,12 +52,31 @@
                 )
 
 
+def times_y(rows, y_all):
+    return lax.dot_general(
+        rows, y_all, (((1,), (1,)), ((), ())), preferred_element_type=jnp.float32
+    )
+
+
+def products_kernel(dx_ref, y_ref, *refs):
+    out_ref = refs[-1]
+    series_x = dx_ref.shape[0]
+    series_y, tile, channels = y_ref.shape
+    y_all = y_ref[...].reshape(series_y * tile, channels)
+    for m in range(series_x):
+        both = times_y(dx_ref[m], y_all)
+        for n in range(series_y):
+            out_ref[m * series_y + n] = both[:, n * tile : (n + 1) * tile]
+        if len(refs) > 1:
+            both = times_y(refs[0][m].astype(jnp.bfloat16), y_all)
+            for n in range(series_y):
+                out_ref[m * series_y + n, 0:1, :] = both[0:1, n * tile : (n + 1) * tile]
+
+
 def tick_kernel(at, last, *refs):
-    start_ref, dx_ref, y_ref, bottom_ref, before_ref, left_ref, *refs = refs
-    if at == 0:
-        head_ref, received_ref, *refs = refs
-    else:
-        row_ref, *refs = refs
+    start_ref, products_ref, bottom_ref, before_ref, left_ref, *refs = refs
+    if at == 0:
+        dx_ref, y_ref, head_ref, received_ref, *refs = refs
     earlier_refs = []
     if last:
         earlier_refs, refs = refs[:at], refs[at:]
@@ -66,10 +85,11 @@
         after_ref, *refs = refs
     if at == 0:
         row_ref, *refs = refs
-    (products_ref,) = refs
-    series_x, block_len, channels = dx_ref.shape
-    series_y, tile, _ = y_ref.shape
-    pairs = series_x * series_y
+    (ones_ref,) = refs
+    pairs, block_len, tile = products_ref.shape
+    if at == 0:
+        series_x, _, channels = dx_ref.shape
+        series_y = y_ref.shape[0]
     levels = block_len // tile
     groups = tile // SUB
     at_start = start_ref[0] == 1
@@ -78,28 +98,21 @@
         for m in range(series_x):
             jump = head_ref[m] - received_ref[m].astype(jnp.float32)
             row_ref[m] = jnp.where(at_start, dx_ref[m, 0:SUB, :].astype(jnp.float32), jump)
-    y_all = y_ref[...].reshape(series_y * tile, channels)
-    for m in range(series_x):
-        both = lax.dot_general(
-            dx_ref[m], y_all, (((1,), (1,)), ((), ())), preferred_element_type=jnp.float32
-        )
-        for n in range(series_y):
-            products_ref[m * series_y + n] = both[:, n * tile : (n + 1) * tile]
-        both = lax.dot_general(
-            row_ref[m].astype(jnp.bfloat16),
-            y_all,
-            (((1,), (1,)), ((), ())),
-            preferred_element_type=jnp.float32,
-        )
-        for n in range(series_y):
-            products_ref[m * series_y + n, 0:1, :] = both[0:1, n * tile : (n + 1) * tile]
+    patch = [None] * pairs
+    if at == 0:
+        y_all = y_ref[...].reshape(series_y * tile, channels)
+        for m in range(series_x):
+            both = times_y(row_ref[m].astype(jnp.bfloat16), y_all)
+            for n in range(series_y):
+                seam = both[0:1, n * tile : (n + 1) * tile]
+                patch[m * series_y + n] = jnp.broadcast_to(seam, (SUB, tile))
 
     row = lax.broadcasted_iota(jnp.int32, (2 * tile, tile), 0) % tile
     col = lax.broadcasted_iota(jnp.int32, (2 * tile, tile), 1)
     strict = (row < col).astype(jnp.float32).astype(jnp.bfloat16)
     inclusive = (row <= col).astype(jnp.float32).astype(jnp.bfloat16)
-    ones = jnp.ones((2 * tile, tile), jnp.bfloat16)
-    edge_sums = jnp.concatenate([strict, inclusive], axis=1)
+    ones_ref[:, :tile] = strict
+    ones_ref[:, tile:] = inclusive
     sub = lax.broadcasted_iota(jnp.int32, (SUB, tile), 0)
     lane = lax.broadcasted_iota(jnp.int32, (SUB, tile), 1)
 
@@ -142,17 +155,17 @@
             end.append(jnp.broadcast_to(left[-1][SUB - 1 : SUB, :], (SUB, tile)))
         node = [[e + bottom_shift[p] for e in edge[p]] for p in range(pairs)]
         for sweep in range(PASSES):
-            weighted = [
-                [
-                    node[p][j] * products_ref[p, pl.ds(r * tile + j, SUB, stride=groups), :]
-                    for j in range(groups)
-                ]
-                for p in range(pairs)
-            ]
+            weighted = [[] for _ in range(pairs)]
+            for p in range(pairs):
+                for j in range(groups):
+                    incr = products_ref[p, pl.ds(r * tile + j, SUB, stride=groups), :]
+                    if at == 0 and r == 0 and j == 0:
+                        incr = jnp.where(sub == 0, patch[p], incr)
+                    weighted[p].append(node[p][j] * incr)
             if sweep == PASSES - 1:
                 break
             for p in range(pairs):
-                along = dot(two_halves(jnp.concatenate(weighted[p], axis=0)), strict)
+                along = dot(two_halves(jnp.concatenate(weighted[p], axis=0)), ones_ref[:, :tile])
                 along = [along[j * SUB : (j + 1) * SUB] for j in range(groups)]
                 running = [None, along[0]]
                 for j in range(1, groups):
@@ -166,10 +179,12 @@
             while len(column) > 1:
                 column = [a + b for a, b in zip(column[::2], column[1::2])]
             column = over_sublanes(column[0])
-            sums = dot(two_halves(column), edge_sums)
+            sums = dot(two_halves(column), ones_ref[...])
             lift = end[p] - corner[p]
-            rows = dot(two_halves(jnp.concatenate(weighted[p], axis=0)), ones)
-            rows = [rows[j * SUB : (j + 1) * SUB] for j in range(groups)]
+            rows = [
+                jnp.broadcast_to(jnp.sum(x, axis=1, keepdims=True), (SUB, tile))
+                for x in weighted[p]
+            ]
             running = [rows[0]]
             for j in range(1, groups):
                 running.append(running[-1] + rows[j])
@@ -216,9 +231,22 @@
     )(x_path, x_anchor, left_in)
 
 
-def tick(at, last, start, dx, y, bottom, before, left, first, tops):
-    pairs, tile = bottom.shape
-    series_x, block_len, channels = dx.shape
+def all_products(dx, y, rows):
+    series_x, block_len, _ = dx.shape
+    series_y, tile, _ = y.shape
+    pairs = series_x * series_y
+    return pl.pallas_call(
+        products_kernel,
+        out_shape=jax.ShapeDtypeStruct((pairs, block_len, tile), jnp.float32),
+        in_specs=[VMEM] * (2 + len(rows)),
+        out_specs=VMEM,
+        compiler_params=pltpu.CompilerParams(vmem_limit_bytes=VMEM_BYTES),
+        name="products",
+    )(dx, y, *rows)
+
+
+def tick(at, last, start, products, bottom, before, left, first, tops):
+    pairs, block_len, tile = products.shape
     edge = jax.ShapeDtypeStruct((pairs, tile), jnp.float32)
     if last:
         shapes = [
@@ -229,17 +257,17 @@
     else:
         shapes = [jax.ShapeDtypeStruct(left.shape, jnp.float32), edge, edge]
     if at == 0:
-        shapes.append(jax.ShapeDtypeStruct((series_x, SUB, channels), jnp.float32))
-    specs = [pl.BlockSpec(memory_space=pltpu.SMEM)] + [VMEM] * (5 + len(first))
+        shapes.append(jax.ShapeDtypeStruct(first[2].shape, jnp.float32))
+    specs = [pl.BlockSpec(memory_space=pltpu.SMEM)] + [VMEM] * (4 + len(first))
     return pl.pallas_call(
         functools.partial(tick_kernel, at, last),
         out_shape=tuple(shapes),
         in_specs=specs,
         out_specs=(VMEM,) * len(shapes),
-        scratch_shapes=[pltpu.VMEM((pairs, block_len, tile), jnp.float32)],
+        scratch_shapes=[pltpu.VMEM((2 * tile, 2 * tile), jnp.bfloat16)],
         compiler_params=pltpu.CompilerParams(vmem_limit_bytes=VMEM_BYTES),
         name="tick",
-    )(start, dx, y, bottom, before, left, *first)
+    )(start, products, bottom, before, left, *first)
 
 
 def local(x_path, x_anchor, y_steps, left_in, bottom_in, corner_in):
@@ -251,18 +279,20 @@
     dx, left, head = prepare(x_path, x_anchor, left_in, tile)
     y_now, bottom = y_steps, bottom_in
     previous = jnp.broadcast_to(corner_in, bottom_in.shape)
-    first, tops = [head, received], []
+    first, tops = [dx, y_steps, head, received], []
+    products = all_products(dx, y_steps, [])
     for t in range(TICKS):
         last = t == TICKS - 1
-        left, top, *rest = tick(t, last, start, dx, y_now, bottom, previous, left, first, tops)
+        left, top, *rest = tick(t, last, start, products, bottom, previous, left, first, tops)
         if last:
             return left, top
         tops.append(top)
         previous = rest[0]
         if t == 0:
-            first = [rest[1]]
+            rows, first = [rest[1]], []
         bottom = shifted(top, "tm", 1)
         y_now = y_next
+        products = all_products(dx, y_now, rows)
         if t + 2 < TICKS:
             y_now, _ = lax.optimization_barrier((y_now, top))
             y_next = passed_along(y_now, "tm", 1)

time: 69.4 us -> 68.4 us (0.986)
  waiting for transfers between devices: 26.6 us -> 22.1 us
  Pallas kernels: 22.3 us -> 23.9 us
  starting transfers between devices: 15.6 us -> 16.6 us
  local copies, waits for them, and re-layouts: 3.3 us -> 4.03 us
    ppermute x6, waiting for transfers between devices: 26.6 us -> 22.1 us  [shifted(): return lax.ppermute(x, axis, pairs)]
    pallas_call x0 -> x6, Pallas kernels: none -> 3.44 us  [all_products(): pl.pallas_call(products_kernel, out_shape=jax.ShapeDtypeStruct((pairs, bl...]
    pallas_call x6, Pallas kernels: 21.4 us -> 19.5 us  [tick(): pl.pallas_call(functools.partial(tick_kernel, at, last), out_shape=tuple(...]
    ppermute x6, starting transfers between devices: 13.2 us -> 14.2 us  [shifted(): return lax.ppermute(x, axis, pairs)]
    unnamed x12, local copies, waits for them, and re-layouts: 2.51 us -> 3.23 us
  transfers between devices with their start and end apart: 11 -> 11, of which waited for: 6 -> 6; matrix products, arithmetic and copies ran while one was open for 1% -> 1% of each run, Pallas kernels for 27% -> 30%
where the time goes in v2:
time: 68.4 us; the launch traced here: 67.5 us
  Pallas kernels  23.9 us (35%)
  waiting for transfers between devices  22.1 us (32%)
  starting transfers between devices  16.6 us (24%)
  local copies, waits for them, and re-layouts  4.03 us (6%)
  between operations  0.84 us (1%)
    ppermute x6, waiting for transfers between devices, shifted(): return lax.ppermute(x, axis, pairs)  22.1 us
    pallas_call x6, Pallas kernels, tick(): pl.pallas_call(functools.partial(tick_kernel, at, last), out_shape=tuple(...  19.5 us
    ppermute x6, starting transfers between devices, shifted(): return lax.ppermute(x, axis, pairs)  14.2 us
    pallas_call x6, Pallas kernels, all_products(): pl.pallas_call(products_kernel, out_shape=jax.ShapeDtypeStruct((pairs, bl...  3.44 us
    unnamed x12, local copies, waits for them, and re-layouts  3.23 us
    ppermute x5, starting transfers between devices, passed_along(): return lax.ppermute(x, axis, [(i, (i + by) % count) for i in range(count)])  2.42 us
  transfers between devices with their start and end apart: 11, of which 6 were waited for; matrix products, arithmetic and copies ran while one was open for 1% of the time, Pallas kernels for 30%

profile of v2, /device:TPU:24, one launch (start us, length us, event | category | flops | bytes accessed | tf_op | source)
XLA Modules:
  0.0 67.5 jit_solution(13689319230209355872)
XLA Ops:
  0.6 1.6 %collective-permute-start = (bf16[2,128,512]{2,1,0:T(8,128)(2,1)}, bf16[2,128,512]{2,1,0:T(8,128)(2,1)S(1)}, u32[]{:S(2)}, u32[]{:S(2)}) collective-permute-start(bf16[2,128,512]{2,1,0:T(8,128)(2,1)} %refs_6_.1), channel_id=1, source_target_pairs={{0,4},{4,8},{8,12},{12,16},{16,20},{20,24},{24,28},{28,0},{1,5},{5... | collective-permute-start | bytes 786440 | tf_op jit(solution)/shard_map/ppermute | solution.py:25
  2.2 0.7 %slice.3 = bf16[2,1,512]{2,1,0:T(2,128)(2,1)S(1)} slice(bf16[2,512,512]{2,1,0:T(8,128)(2,1)} %x_ref.1), slice={[0:2], [511:512], [0:512]} | slice | bytes 4096 | tf_op jit(solution)/shard_map/slice | solution.py:277
  2.9 1.9 %collective-permute-start.1 = (bf16[2,1,512]{2,1,0:T(2,128)(2,1)S(1)}, bf16[2,1,512]{2,1,0:T(2,128)(2,1)S(1)}, u32[]{:S(2)}, u32[]{:S(2)}) collective-permute-start(bf16[2,1,512]{2,1,0:T(2,128)(2,1)S(1)} %slice.3), channel_id=1, source_target_pairs={{0,4},{4,8},{8,12},{12,16},{16,20},{20,24},{24,28},{1,5},{5,9},{9,... | collective-permute-start | bytes 6152 | tf_op jit(solution)/shard_map/ppermute | solution.py:20
  5.6 1.2 %copy-done = bf16[2,512,512]{2,1,0:T(8,128)(2,1)S(1)} copy-done((bf16[2,512,512]{2,1,0:T(8,128)(2,1)S(1)}, bf16[2,512,512]{2,1,0:T(8,128)(2,1)}, u32[]{:S(2)}) %copy-start) | copy-done | bytes 1048600
  6.8 0.9 %prep.1 = (bf16[2,512,512]{2,1,0:T(8,128)(2,1)S(1)}, f32[4,4,16,8,128]{4,3,2,1,0:T(8,128)S(1)}, f32[2,8,512]{2,1,0:T(8,128)S(1)}) custom-call(bf16[2,512,512]{2,1,0:T(8,128)(2,1)S(1)} %copy-done, bf16[2,512]{1,0:T(2,128)(2,1)S(1)} %copy-done.3, f32[4,512]{1,0:T(4,128)S(1)} %copy-done.2), custom_call_target="tpu_custom_call" | custom-call | tf_op jit(solution)/shard_map/prep/pallas_call | solution.py:220
  8.2 1.7 %collective-permute-done.1.refs_8_ = bf16[2,1,512]{2,1,0:T(2,128)(2,1)S(1)} collective-permute-done((bf16[2,1,512]{2,1,0:T(2,128)(2,1)S(1)}, bf16[2,1,512]{2,1,0:T(2,128)(2,1)S(1)}, u32[]{:S(2)}, u32[]{:S(2)}) %collective-permute-start.1) | collective-permute-done | bytes 2080 | tf_op jit(solution)/shard_map/ppermute | solution.py:20
  10.7 0.7 %copy-done.4 = f32[4,128]{1,0:T(4,128)S(1)} copy-done((f32[4,128]{1,0:T(4,128)S(1)}, f32[4,128]{1,0:T(4,128)}, u32[]{:S(2)}) %copy-start.4) | copy-done | bytes 2072
  11.3 3.2 %tick.6 = (f32[4,4,16,8,128]{4,3,2,1,0:T(8,128)S(1)}, f32[4,128]{1,0:T(4,128)S(1)}, f32[4,128]{1,0:T(4,128)S(1)}, f32[2,8,512]{2,1,0:T(8,128)S(1)}) custom-call(s32[1]{0:T(128)} %bitcast.refs_0_, f32[4,512,128]{2,1,0:T(8,128)S(1)} %products.6.refs_1_, f32[4,128]{1,0:T(4,128)S(1)} %copy-done.4, f32[4,128]{1,0:T(4,128)S(1)} %broadcast_in_dim.8.refs_3_, ...), custom_call_target="tpu_custom_call" | custom-call | tf_op jit(solution)/shard_map/tick/pallas_call | solution.py:262
  14.6 0.7 collective-permute-start.2
  15.3 2.7 %collective-permute-start.3 = (f32[4,128]{1,0:T(4,128)S(1)}, f32[4,128]{1,0:T(4,128)S(1)}, u32[]{:S(2)}, u32[]{:S(2)}) collective-permute-start(f32[4,128]{1,0:T(4,128)S(1)} %get-tuple-element.28.refs_5_), channel_id=1, source_target_pairs={{0,4},{4,8},{8,12},{12,16},{16,20},{20,24},{24,28},{1,5},{5,9},{9,... | collective-permute-start | bytes 6152 | tf_op jit(solution)/shard_map/ppermute | solution.py:20
  18.6 4.2 %collective-permute-done.3.refs_2_ = f32[4,128]{1,0:T(4,128)S(1)} collective-permute-done((f32[4,128]{1,0:T(4,128)S(1)}, f32[4,128]{1,0:T(4,128)S(1)}, u32[]{:S(2)}, u32[]{:S(2)}) %collective-permute-start.3) | collective-permute-done | bytes 2080 | tf_op jit(solution)/shard_map/ppermute | solution.py:20
  22.8 3.1 %tick.7 = (f32[4,4,16,8,128]{4,3,2,1,0:T(8,128)S(1)}, f32[4,128]{1,0:T(4,128)S(1)}, f32[4,128]{1,0:T(4,128)S(1)}) custom-call(s32[1]{0:T(128)} %bitcast.refs_0_, f32[4,512,128]{2,1,0:T(8,128)S(1)} %products.7.refs_1_, f32[4,128]{1,0:T(4,128)S(1)} %collective-permute-done.3.refs_2_, f32[4,128]{1,0:T(4,128)S(1)} %get-tuple-element.31.refs_3_, ...), custom_call_target="tpu_custom_call" | custom-call | tf_op jit(solution)/shard_map/tick/pallas_call | solution.py:262
  26.0 2.2 %collective-permute-start.5 = (f32[4,128]{1,0:T(4,128)S(1)}, f32[4,128]{1,0:T(4,128)S(1)}, u32[]{:S(2)}, u32[]{:S(2)}) collective-permute-start(f32[4,128]{1,0:T(4,128)S(1)} %get-tuple-element.33.refs_6_), channel_id=1, source_target_pairs={{0,4},{4,8},{8,12},{12,16},{16,20},{20,24},{24,28},{1,5},{5,9},{9,... | collective-permute-start | bytes 6152 | tf_op jit(solution)/shard_map/ppermute | solution.py:20
  28.8 4.5 %collective-permute-done.5.refs_2_ = f32[4,128]{1,0:T(4,128)S(1)} collective-permute-done((f32[4,128]{1,0:T(4,128)S(1)}, f32[4,128]{1,0:T(4,128)S(1)}, u32[]{:S(2)}, u32[]{:S(2)}) %collective-permute-start.5) | collective-permute-done | bytes 2080 | tf_op jit(solution)/shard_map/ppermute | solution.py:20
  33.3 3.1 %tick.8 = (f32[4,4,16,8,128]{4,3,2,1,0:T(8,128)S(1)}, f32[4,128]{1,0:T(4,128)S(1)}, f32[4,128]{1,0:T(4,128)S(1)}) custom-call(s32[1]{0:T(128)} %bitcast.refs_0_, f32[4,512,128]{2,1,0:T(8,128)S(1)} %products.8.refs_1_, f32[4,128]{1,0:T(4,128)S(1)} %collective-permute-done.5.refs_2_, f32[4,128]{1,0:T(4,128)S(1)} %get-tuple-element.35.refs_3_, ...), custom_call_target="tpu_custom_call" | custom-call | tf_op jit(solution)/shard_map/tick/pallas_call | solution.py:262
  36.5 2.8 %collective-permute-start.7 = (f32[4,128]{1,0:T(4,128)S(1)}, f32[4,128]{1,0:T(4,128)S(1)}, u32[]{:S(2)}, u32[]{:S(2)}) collective-permute-start(f32[4,128]{1,0:T(4,128)S(1)} %get-tuple-element.37.refs_7_), channel_id=1, source_target_pairs={{0,4},{4,8},{8,12},{12,16},{16,20},{20,24},{24,28},{1,5},{5,9},{9,... | collective-permute-start | bytes 6152 | tf_op jit(solution)/shard_map/ppermute | solution.py:20
  39.9 3.9 %collective-permute-done.7.refs_2_ = f32[4,128]{1,0:T(4,128)S(1)} collective-permute-done((f32[4,128]{1,0:T(4,128)S(1)}, f32[4,128]{1,0:T(4,128)S(1)}, u32[]{:S(2)}, u32[]{:S(2)}) %collective-permute-start.7) | collective-permute-done | bytes 2080 | tf_op jit(solution)/shard_map/ppermute | solution.py:20
  43.8 3.1 %tick.9 = (f32[4,4,16,8,128]{4,3,2,1,0:T(8,128)S(1)}, f32[4,128]{1,0:T(4,128)S(1)}, f32[4,128]{1,0:T(4,128)S(1)}) custom-call(s32[1]{0:T(128)} %bitcast.refs_0_, f32[4,512,128]{2,1,0:T(8,128)S(1)} %products.9.refs_1_, f32[4,128]{1,0:T(4,128)S(1)} %collective-permute-done.7.refs_2_, f32[4,128]{1,0:T(4,128)S(1)} %get-tuple-element.39.refs_3_, ...), custom_call_target="tpu_custom_call" | custom-call | tf_op jit(solution)/shard_map/tick/pallas_call | solution.py:262
  47.0 2.7 %collective-permute-start.9 = (f32[4,128]{1,0:T(4,128)S(1)}, f32[4,128]{1,0:T(4,128)S(1)}, u32[]{:S(2)}, u32[]{:S(2)}) collective-permute-start(f32[4,128]{1,0:T(4,128)S(1)} %get-tuple-element.41.refs_8_), channel_id=1, source_target_pairs={{0,4},{4,8},{8,12},{12,16},{16,20},{20,24},{24,28},{1,5},{5,9},{9,... | collective-permute-start | bytes 6152 | tf_op jit(solution)/shard_map/ppermute | solution.py:20
  50.3 4.0 %collective-permute-done.9.refs_2_ = f32[4,128]{1,0:T(4,128)S(1)} collective-permute-done((f32[4,128]{1,0:T(4,128)S(1)}, f32[4,128]{1,0:T(4,128)S(1)}, u32[]{:S(2)}, u32[]{:S(2)}) %collective-permute-start.9) | collective-permute-done | bytes 2080 | tf_op jit(solution)/shard_map/ppermute | solution.py:20
  54.3 3.1 %tick.10 = (f32[4,4,16,8,128]{4,3,2,1,0:T(8,128)S(1)}, f32[4,128]{1,0:T(4,128)S(1)}, f32[4,128]{1,0:T(4,128)S(1)}) custom-call(s32[1]{0:T(128)} %bitcast.refs_0_, f32[4,512,128]{2,1,0:T(8,128)S(1)} %products.11.refs_1_, f32[4,128]{1,0:T(4,128)S(1)} %collective-permute-done.9.refs_2_, f32[4,128]{1,0:T(4,128)S(1)} %get-tuple-element.43.refs_3_, ...), custom_call_target="tpu_custom_call" | custom-call | tf_op jit(solution)/shard_map/tick/pallas_call | solution.py:262
  57.4 1.9 %collective-permute-start.10 = (f32[4,128]{1,0:T(4,128)S(1)}, f32[4,128]{1,0:T(4,128)S(1)}, u32[]{:S(2)}, u32[]{:S(2)}) collective-permute-start(f32[4,128]{1,0:T(4,128)S(1)} %get-tuple-element.45.refs_9_), channel_id=1, source_target_pairs={{0,4},{4,8},{8,12},{12,16},{16,20},{20,24},{24,28},{1,5},{5,9},{9,... | collective-permute-start | bytes 6152 | tf_op jit(solution)/shard_map/ppermute | solution.py:20
  60.0 3.8 %collective-permute-done.10.refs_2_ = f32[4,128]{1,0:T(4,128)S(1)} collective-permute-done((f32[4,128]{1,0:T(4,128)S(1)}, f32[4,128]{1,0:T(4,128)S(1)}, u32[]{:S(2)}, u32[]{:S(2)}) %collective-permute-start.10) | collective-permute-done | bytes 2080 | tf_op jit(solution)/shard_map/ppermute | solution.py:20
  63.8 3.7 %tick.11 = (f32[4,512]{1,0:T(4,128)}, f32[4,768]{1,0:T(4,128)}) custom-call(s32[1]{0:T(128)} %bitcast.refs_0_, f32[4,512,128]{2,1,0:T(8,128)S(1)} %products.10.refs_1_, f32[4,128]{1,0:T(4,128)S(1)} %collective-permute-done.10.refs_2_, f32[4,128]{1,0:T(4,128)S(1)} %get-tuple-element.46.refs_3_, f32[4,4,16,8,128]{4,3,2,1,0:T(8,128)S(1)} %get-tuple-element.47.refs_4_, ...), custom_call_target="tpu_custom_call" | custom-call | tf_op jit(solution)/shard_map/tick/pallas_call | solution.py:262
  (25 shorter events, 5.0 us)
Async XLA Ops:
  0.6 4.3 %copy-start.2 = (f32[4,512]{1,0:T(4,128)S(1)}, f32[4,512]{1,0:T(4,128)}, u32[]{:S(2)}) copy-start(f32[4,512]{1,0:T(4,128)} %left_ref.1) | copy-start | bytes 24580
  0.6 13.9 %collective-permute-start = (bf16[2,128,512]{2,1,0:T(8,128)(2,1)}, bf16[2,128,512]{2,1,0:T(8,128)(2,1)S(1)}, u32[]{:S(2)}, u32[]{:S(2)}) collective-permute-start(bf16[2,128,512]{2,1,0:T(8,128)(2,1)} %refs_6_.1), channel_id=1, source_target_pairs={{0,4},{4,8},{8,12},{12,16},{16,20},{20,24},{24,28},{28,0},{1,5},{5... | collective-permute-start | bytes 786440 | tf_op jit(solution)/shard_map/ppermute | solution.py:25
  2.9 7.0 %collective-permute-start.1 = (bf16[2,1,512]{2,1,0:T(2,128)(2,1)S(1)}, bf16[2,1,512]{2,1,0:T(2,128)(2,1)S(1)}, u32[]{:S(2)}, u32[]{:S(2)}) collective-permute-start(bf16[2,1,512]{2,1,0:T(2,128)(2,1)S(1)} %slice.3), channel_id=1, source_target_pairs={{0,4},{4,8},{8,12},{12,16},{16,20},{20,24},{24,28},{1,5},{5,9},{9,... | collective-permute-start | bytes 6152 | tf_op jit(solution)/shard_map/ppermute | solution.py:20
  4.9 0.7 %copy-start.3 = (bf16[2,512]{1,0:T(2,128)(2,1)S(1)}, bf16[2,512]{1,0:T(2,128)(2,1)}, u32[]{:S(2)}) copy-start(bf16[2,512]{1,0:T(2,128)(2,1)} %anchor_ref.1) | copy-start | bytes 6148
  5.5 1.2 %copy-start = (bf16[2,512,512]{2,1,0:T(8,128)(2,1)S(1)}, bf16[2,512,512]{2,1,0:T(8,128)(2,1)}, u32[]{:S(2)}) copy-start(bf16[2,512,512]{2,1,0:T(8,128)(2,1)} %x_ref.1) | copy-start | bytes 3145732
  6.8 1.0 %copy-start.1 = (bf16[2,128,512]{2,1,0:T(8,128)(2,1)S(1)}, bf16[2,128,512]{2,1,0:T(8,128)(2,1)}, u32[]{:S(2)}) copy-start(bf16[2,128,512]{2,1,0:T(8,128)(2,1)} %refs_6_.1) | copy-start | bytes 786436
  9.9 0.7 copy-start.5
  10.7 0.7 %copy-start.4 = (f32[4,128]{1,0:T(4,128)S(1)}, f32[4,128]{1,0:T(4,128)}, u32[]{:S(2)}) copy-start(f32[4,128]{1,0:T(4,128)} %refs_2_.1) | copy-start | bytes 6148
  14.6 11.3 %collective-permute-start.2 = (bf16[2,128,512]{2,1,0:T(8,128)(2,1)S(1)}, bf16[2,128,512]{2,1,0:T(8,128)(2,1)S(1)}, u32[]{:S(2)}, u32[]{:S(2)}) collective-permute-start(bf16[2,128,512]{2,1,0:T(8,128)(2,1)S(1)} %collective-permute-done.y_ref), channel_id=1, source_target_pairs={{0,4},{4,8},{8,12},{12,16},{16,20},{20,24},{24,28},{28,0},{1,5},{5... | collective-permute-start | bytes 786440 | tf_op jit(solution)/shard_map/ppermute | solution.py:25
  15.3 7.5 %collective-permute-start.3 = (f32[4,128]{1,0:T(4,128)S(1)}, f32[4,128]{1,0:T(4,128)S(1)}, u32[]{:S(2)}, u32[]{:S(2)}) collective-permute-start(f32[4,128]{1,0:T(4,128)S(1)} %get-tuple-element.28.refs_5_), channel_id=1, source_target_pairs={{0,4},{4,8},{8,12},{12,16},{16,20},{20,24},{24,28},{1,5},{5,9},{9,... | collective-permute-start | bytes 6152 | tf_op jit(solution)/shard_map/ppermute | solution.py:20
  25.9 10.5 %collective-permute-start.4 = (bf16[2,128,512]{2,1,0:T(8,128)(2,1)S(1)}, bf16[2,128,512]{2,1,0:T(8,128)(2,1)S(1)}, u32[]{:S(2)}, u32[]{:S(2)}) collective-permute-start(bf16[2,128,512]{2,1,0:T(8,128)(2,1)S(1)} %collective-permute-done.2.y_ref), channel_id=1, source_target_pairs={{0,4},{4,8},{8,12},{12,16},{16,20},{20,24},{24,28},{28,0},{1,5},{5... | collective-permute-start | bytes 786440 | tf_op jit(solution)/shard_map/ppermute | solution.py:25
  26.0 7.3 %collective-permute-start.5 = (f32[4,128]{1,0:T(4,128)S(1)}, f32[4,128]{1,0:T(4,128)S(1)}, u32[]{:S(2)}, u32[]{:S(2)}) collective-permute-start(f32[4,128]{1,0:T(4,128)S(1)} %get-tuple-element.33.refs_6_), channel_id=1, source_target_pairs={{0,4},{4,8},{8,12},{12,16},{16,20},{20,24},{24,28},{1,5},{5,9},{9,... | collective-permute-start | bytes 6152 | tf_op jit(solution)/shard_map/ppermute | solution.py:20
  36.4 10.5 %collective-permute-start.6 = (bf16[2,128,512]{2,1,0:T(8,128)(2,1)S(1)}, bf16[2,128,512]{2,1,0:T(8,128)(2,1)S(1)}, u32[]{:S(2)}, u32[]{:S(2)}) collective-permute-start(bf16[2,128,512]{2,1,0:T(8,128)(2,1)S(1)} %collective-permute-done.4.y_ref), channel_id=1, source_target_pairs={{0,4},{4,8},{8,12},{12,16},{16,20},{20,24},{24,28},{28,0},{1,5},{5... | collective-permute-start | bytes 786440 | tf_op jit(solution)/shard_map/ppermute | solution.py:25
  36.5 7.3 %collective-permute-start.7 = (f32[4,128]{1,0:T(4,128)S(1)}, f32[4,128]{1,0:T(4,128)S(1)}, u32[]{:S(2)}, u32[]{:S(2)}) collective-permute-start(f32[4,128]{1,0:T(4,128)S(1)} %get-tuple-element.37.refs_7_), channel_id=1, source_target_pairs={{0,4},{4,8},{8,12},{12,16},{16,20},{20,24},{24,28},{1,5},{5,9},{9,... | collective-permute-start | bytes 6152 | tf_op jit(solution)/shard_map/ppermute | solution.py:20
  46.9 12.4 %collective-permute-start.8 = (bf16[2,128,512]{2,1,0:T(8,128)(2,1)S(1)}, bf16[2,128,512]{2,1,0:T(8,128)(2,1)S(1)}, u32[]{:S(2)}, u32[]{:S(2)}) collective-permute-start(bf16[2,128,512]{2,1,0:T(8,128)(2,1)S(1)} %collective-permute-done.6.y_ref), channel_id=1, source_target_pairs={{0,4},{4,8},{8,12},{12,16},{16,20},{20,24},{24,28},{28,0},{1,5},{5... | collective-permute-start | bytes 786440 | tf_op jit(solution)/shard_map/ppermute | solution.py:25
  47.0 7.3 %collective-permute-start.9 = (f32[4,128]{1,0:T(4,128)S(1)}, f32[4,128]{1,0:T(4,128)S(1)}, u32[]{:S(2)}, u32[]{:S(2)}) collective-permute-start(f32[4,128]{1,0:T(4,128)S(1)} %get-tuple-element.41.refs_8_), channel_id=1, source_target_pairs={{0,4},{4,8},{8,12},{12,16},{16,20},{20,24},{24,28},{1,5},{5,9},{9,... | collective-permute-start | bytes 6152 | tf_op jit(solution)/shard_map/ppermute | solution.py:20
  57.4 6.4 %collective-permute-start.10 = (f32[4,128]{1,0:T(4,128)S(1)}, f32[4,128]{1,0:T(4,128)S(1)}, u32[]{:S(2)}, u32[]{:S(2)}) collective-permute-start(f32[4,128]{1,0:T(4,128)S(1)} %get-tuple-element.45.refs_9_), channel_id=1, source_target_pairs={{0,4},{4,8},{8,12},{12,16},{16,20},{20,24},{24,28},{1,5},{5,9},{9,... | collective-permute-start | bytes 6152 | tf_op jit(solution)/shard_map/ppermute | solution.py:20
